TPU v7x, 32 devices: a whole 2x2x4 slice. The times are simulated.
32 devices in a mesh: seq: 8 (over z, x), dp: 4 (over y, core).
Axes of the slice: x: 2, y: 2, z: 4, core: 2. Of those that a mesh axis runs over, the one named last changes fastest.
Arguments:
- bases: int32 [4, 16384], P('dp', 'seq'), may hold values from 0 to 3
- stem_table: bfloat16 [60, 256], replicated, may hold values from -1.5 to 1.5
- first_conv_taps: bfloat16 [3, 256, 128], replicated, may hold values from -0.21875 to 0.21875
- first_projection_weight: bfloat16 [128, 256], replicated, may hold values from -0.5 to 0.5
- second_conv_taps: bfloat16 [3, 256, 128], replicated, may hold values from -0.21875 to 0.21875
- second_projection_weight: bfloat16 [128, 256], replicated, may hold values from -0.5 to 0.5
- bin_weight: bfloat16 [1536, 256], P('seq'), may hold values from -0.375 to 0.375
- cotangent: bfloat16 [4, 1536, 128], P('dp', 'seq'), may hold values from -96 to 96
Outputs:
- predictions: bfloat16 [4, 1536, 128], P('dp', 'seq')
- saliency: float32 [4, 4, 16384], P('dp', None, 'seq')
- conv_one_grad: float32 [3, 256, 128], replicated
- proj_one_grad: float32 [128, 256], replicated
- conv_two_grad: float32 [3, 256, 128], replicated
- proj_two_grad: float32 [128, 256], replicated
- bin_weight_grad: float32 [1536, 256], P('seq')
All inputs are finite; a program needn't handle non-finite values.
Results may differ from a plain program's by a relative error of at most 0.015.
Values may be sent and summed in bfloat16 or wider, within the bound.
A program may use at most 64 MiB of HBM per device.

v0:
```python
import jax
import jax.numpy as jnp
from jax import lax
from jax.sharding import PartitionSpec as P

STEM = 15
POOL = 128


def passed_along(value, axis, steps):
    count = lax.axis_size(axis)
    first, last = (max(0, -steps), min(count, count - steps))
    return lax.ppermute(value, axis, [(source, source + steps) for source in range(first, last)])


def with_halo(cells, sides, width):
    for axis, dim in sides:
        count = lax.axis_size(axis)
        ends = count - 1
        head = lax.slice_in_dim(cells, 0, width, axis=dim)
        tail = lax.slice_in_dim(cells, cells.shape[dim] - width, cells.shape[dim], axis=dim)
        cells = jnp.concatenate(
            [
                lax.ppermute(tail, axis, [(i, (i + 1) % count) for i in range(ends)]),
                cells,
                lax.ppermute(head, axis, [((i + 1) % count, i) for i in range(ends)]),
            ],
            axis=dim,
        )
    return cells


def gelu_exact(value):
    return 0.5 * value * (1.0 + jax.scipy.special.erf(value * 0.7071067811865476))


def gelu_slope(value):
    return (
        0.5 * (1.0 + jax.scipy.special.erf(value * 0.7071067811865476))
        + value * jnp.exp(-0.5 * value * value) * 0.3989422804014327
    )


def tap_shift(values, hops):
    return passed_along(values, "seq", hops)


def grad_shift(values, hops):
    return passed_along(values, "seq", hops)


def reduce_grads(conv_raw, proj_raw):
    return lax.psum((conv_raw, proj_raw), ("seq", "dp"))


def residual_block_apply(stream, conv_w, proj_w, hops):
    act = gelu_exact(stream.astype(jnp.float32)).astype(jnp.bfloat16)
    before = tap_shift(act, hops)
    after = tap_shift(act, -hops)
    tap_before = jnp.dot(before, conv_w[0], preferred_element_type=jnp.float32).astype(jnp.bfloat16)
    tap_after = jnp.dot(after, conv_w[2], preferred_element_type=jnp.float32).astype(jnp.bfloat16)
    pre = jnp.dot(act, conv_w[1], preferred_element_type=jnp.float32)
    pre = pre + tap_before.astype(jnp.float32) + tap_after.astype(jnp.float32)
    inner = gelu_exact(pre).astype(jnp.bfloat16)
    result = (
        stream.astype(jnp.float32) + jnp.dot(inner, proj_w, preferred_element_type=jnp.float32)
    ).astype(jnp.bfloat16)
    return (result, (stream, act, before, after, pre, inner))


def residual_block_reverse(incoming, saved, conv_w, proj_w, hops):
    stream, act, before, after, pre, inner = saved
    grad_in = incoming.astype(jnp.bfloat16)
    inner_grad = jnp.dot(grad_in, proj_w.T, preferred_element_type=jnp.float32)
    pre_grad = (inner_grad * gelu_slope(pre)).astype(jnp.bfloat16)
    later = grad_shift(pre_grad, -hops)
    earlier = grad_shift(pre_grad, hops)
    proj_raw = jnp.dot(inner.T, grad_in, preferred_element_type=jnp.float32)
    middle = jnp.dot(act.T, pre_grad, preferred_element_type=jnp.float32)
    conv_raw = jnp.stack(
        [
            jnp.dot(before.T, pre_grad, preferred_element_type=jnp.float32),
            middle,
            jnp.dot(after.T, pre_grad, preferred_element_type=jnp.float32),
        ]
    )
    act_grad = jnp.dot(pre_grad, conv_w[1].T, preferred_element_type=jnp.float32)
    act_grad = act_grad + jnp.dot(later, conv_w[0].T, preferred_element_type=jnp.float32)
    act_grad = act_grad + jnp.dot(earlier, conv_w[2].T, preferred_element_type=jnp.float32)
    outgoing = incoming + act_grad * gelu_slope(stream.astype(jnp.float32))
    conv_sum, proj_sum = reduce_grads(conv_raw, proj_raw)
    return (outgoing, conv_sum, proj_sum)


def per_device(
    bases,
    stem_table,
    first_conv_taps,
    first_projection_weight,
    second_conv_taps,
    second_projection_weight,
    bin_weight,
    cotangent,
):
    length = bases.shape[1]
    width = stem_table.shape[1]
    half = STEM // 2
    bins_dev = length // POOL
    scale = float(lax.axis_size("dp") * lax.axis_size("seq") * length) ** (-0.5)
    padded_ids = with_halo(bases[0] + 1, (("seq", 0),), half)
    taps = jnp.stack([padded_ids[k : k + length] for k in range(STEM)], axis=1)
    letters = jnp.arange(1, 5, dtype=jnp.int32)
    codes = (
        (taps[:, :, None] == letters[None, None, :]).astype(jnp.bfloat16).reshape(length, 4 * STEM)
    )
    stem_pre = jnp.dot(codes, stem_table, preferred_element_type=jnp.float32)
    residual_input_level = gelu_exact(stem_pre).astype(jnp.bfloat16)
    residual_after_first, first_block_stash = residual_block_apply(
        residual_input_level, first_conv_taps, first_projection_weight, 1
    )
    residual_after_second, second_block_stash = residual_block_apply(
        residual_after_first, second_conv_taps, second_projection_weight, 2
    )
    pooled = jnp.mean(
        residual_after_second.astype(jnp.float32).reshape(bins_dev, POOL, width), axis=1
    )
    pooled_act = gelu_exact(pooled).astype(jnp.bfloat16)
    cot_rows = cotangent[0]
    gathered = lax.all_gather(pooled_act, "seq", axis=0, tiled=True)
    preds = lax.dot_general(
        bin_weight, gathered, (((1,), (1,)), ((), ())), preferred_element_type=jnp.float32
    ).astype(jnp.bfloat16)
    bin_part = jnp.dot(cot_rows, gathered, preferred_element_type=jnp.float32)
    summed = lax.psum_scatter(
        lax.dot_general(
            cot_rows, bin_weight, (((0,), (0,)), ((), ())), preferred_element_type=jnp.float32
        ),
        "seq",
        scatter_dimension=0,
        tiled=True,
    )
    bin_total = lax.psum(bin_part, "dp")
    pooled_grad = summed * gelu_slope(pooled)
    gradient_after_second = jnp.repeat(pooled_grad / POOL, POOL, axis=0)
    gradient_after_first, conv_two_sum, proj_two_sum = residual_block_reverse(
        gradient_after_second, second_block_stash, second_conv_taps, second_projection_weight, 2
    )
    gradient_input_level, conv_one_sum, proj_one_sum = residual_block_reverse(
        gradient_after_first, first_block_stash, first_conv_taps, first_projection_weight, 1
    )
    stem_grad = (gradient_input_level * gelu_slope(stem_pre)).astype(jnp.bfloat16)
    code_grad = jnp.dot(stem_grad, stem_table.T, preferred_element_type=jnp.float32)
    padded_grad = with_halo(code_grad.astype(jnp.bfloat16), (("seq", 0),), half).astype(
        code_grad.dtype
    )
    total = jnp.zeros((length, 4), jnp.float32)
    for k in range(STEM):
        start = 2 * half - k
        total = total + padded_grad[start : start + length, 4 * k : 4 * k + 4]
    return (
        preds[None],
        total.T[None],
        conv_one_sum * scale,
        proj_one_sum * scale,
        conv_two_sum * scale,
        proj_two_sum * scale,
        bin_total * scale,
    )


def solution(mesh):
    placed = (P("dp", "seq"), P(), P(), P(), P(), P(), P("seq", None), P("dp", "seq", None))
    return jax.shard_map(
        per_device,
        mesh=mesh,
        in_specs=placed,
        out_specs=(P("dp", "seq", None), P("dp", None, "seq"), P(), P(), P(), P(), P("seq", None)),
        check_vma=False,
    )
```

profile of v0, /device:TPU:1, one launch (start us, length us, event | category | flops | bytes accessed | tf_op | source)
XLA Modules:
  0.0 390.5 jit_solution(10875098786086386174)
XLA Ops:
  9.3 4.6 %collective-permute-start = (s32[7]{0:T(128)S(1)}, s32[7]{0:T(128)S(1)}, u32[]{:S(2)}, u32[]{:S(2)}) collective-permute-start(s32[7]{0:T(128)S(1)} %get-tuple-element.30), channel_id=1, source_target_pairs={{0,4},{4,8},{8,12},{12,16},{16,20},{20,24},{24,28},{1,5},{5,9},{9,... | collective-permute-start | bytes 92 | tf_op jit(solution)/shard_map/ppermute | solution.py:24
  16.3 4.3 %collective-permute-start.2 = (bf16[2048,256]{1,0:T(8,128)(2,1)S(1)}, bf16[2048,256]{1,0:T(8,128)(2,1)S(1)}, u32[]{:S(2)}, u32[]{:S(2)}) collective-permute-start(bf16[2048,256]{1,0:T(8,128)(2,1)S(1)} %get-tuple-element.33), channel_id=1, source_target_pairs={{0,4},{4,8},{8,12},{12,16},{16,20},{20,24},{24,28},{1,5},{5,9},{9,... | collective-permute-start | bytes 3145736 | tf_op jit(solution)/shard_map/ppermute | solution.py:13
  20.6 1.3 collective-permute-start.3
  22.4 41.3 %collective-permute-done.2 = bf16[2048,256]{1,0:T(8,128)(2,1)S(1)} collective-permute-done((bf16[2048,256]{1,0:T(8,128)(2,1)S(1)}, bf16[2048,256]{1,0:T(8,128)(2,1)S(1)}, u32[]{:S(2)}, u32[]{:S(2)}) %collective-permute-start.2) | collective-permute-done | bytes 1048608 | tf_op jit(solution)/shard_map/ppermute | solution.py:13
  65.1 2.5 fusion.29
  67.7 8.2 %collective-permute-start.4 = (bf16[2048,256]{1,0:T(8,128)(2,1)}, bf16[2048,256]{1,0:T(8,128)(2,1)S(1)}, u32[]{:S(2)}, u32[]{:S(2)}) collective-permute-start(bf16[2048,256]{1,0:T(8,128)(2,1)} %get-tuple-element.35), channel_id=1, source_target_pairs={{0,8},{4,12},{8,16},{12,20},{16,24},{20,28},{1,9},{5,13},{9,17},{1... | collective-permute-start | bytes 3145736 | tf_op jit(solution)/shard_map/ppermute | solution.py:13
  78.2 1.6 fusion.59
  79.8 19.0 %collective-permute-done.4 = bf16[2048,256]{1,0:T(8,128)(2,1)S(1)} collective-permute-done((bf16[2048,256]{1,0:T(8,128)(2,1)}, bf16[2048,256]{1,0:T(8,128)(2,1)S(1)}, u32[]{:S(2)}, u32[]{:S(2)}) %collective-permute-start.4) | collective-permute-done | bytes 1048608 | tf_op jit(solution)/shard_map/ppermute | solution.py:13
  99.3 3.5 collective-permute-done.5
  102.8 1.4 multiply_convert_fusion.1
  105.4 33.7 %reduce-scatter.2.cloned.1.call-done = f32[16,256]{1,0:T(8,128)} async-done(((f32[128,256]{1,0:T(8,128)}), f32[16,256]{1,0:T(8,128)}) %reduce-scatter.2.cloned.1.call-update) | async-done | bytes 16400 | tf_op jit(solution)/shard_map/reduce_scatter | solution.py:134
  140.0 2.0 fusion.107
  142.1 1.4 fusion.7
  143.4 2.5 convolution_bitcast_fusion.2
  145.9 1.5 fusion.57
  148.7 4.8 %collective-permute-start.7 = (bf16[2048,128]{1,0:T(8,128)(2,1)}, bf16[2048,128]{1,0:T(8,128)(2,1)}, u32[]{:S(2)}, u32[]{:S(2)}) collective-permute-start(bf16[2048,128]{1,0:T(8,128)(2,1)} %fusion.7), channel_id=1, source_target_pairs={{0,8},{4,12},{8,16},{12,20},{16,24},{20,28},{1,9},{5,13},{9,17},{1... | collective-permute-start | bytes 1572872 | tf_op jit(solution)/shard_map/ppermute | solution.py:13
  153.5 28.0 %all_gather.3 = bf16[128,256]{1,0:T(8,128)(2,1)S(1)} all-gather(bf16[16,256]{1,0:T(8,128)(2,1)S(1)} %get-tuple-element.14), channel_id=1, replica_groups=mesh['seq'=8,'dp'=4] {'seq'}, dimensions={0}, use_global_device_ids=true | all-gather | bytes 73728 | tf_op jit(solution)/shard_map/all_gather | solution.py:129
  183.2 1.9 convolution_bitcast_fusion.1
  185.1 1.8 convolution_bitcast_fusion.3
  187.7 1.6 convolution_add_fusion.3
  189.3 2.2 bitcast_add_fusion
  192.7 2.0 fusion.8
  197.2 24.8 %all-reduce.4.cloned.1.call-done = f32[192,256]{1,0:T(8,128)} async-done(((f32[192,256]{1,0:T(8,128)}), f32[192,256]{1,0:T(8,128)}) %all-reduce.4.cloned.1.call-update) | async-done | bytes 196624 | tf_op jit(solution)/shard_map/psum | solution.py:142
  222.0 1.6 broadcast_multiply_fusion.2
  224.9 4.9 %collective-permute-start.9 = (bf16[2048,128]{1,0:T(8,128)(2,1)S(1)}, bf16[2048,128]{1,0:T(8,128)(2,1)}, u32[]{:S(2)}, u32[]{:S(2)}) collective-permute-start(bf16[2048,128]{1,0:T(8,128)(2,1)S(1)} %fusion.8), channel_id=1, source_target_pairs={{0,4},{4,8},{8,12},{12,16},{16,20},{20,24},{24,28},{1,5},{5,9},{9,... | collective-permute-start | bytes 1572872 | tf_op jit(solution)/shard_map/ppermute | solution.py:13
  229.8 1.8 fusion.66
  231.5 133.2 %all-reduce.6.cloned.1.call-done = (f32[3,256,128]{2,1,0:T(8,128)}, f32[128,256]{1,0:T(8,128)}, f32[3,256,128]{2,1,0:T(8,128)}, f32[128,256]{1,0:T(8,128)}) async-done(((f32[3,256,128]{2,1,0:T(8,128)}, f32[128,256]{1,0:T(8,128)}, f32[3,256,128]{2,1,0:T(8,128)}, f32[128,256]{1,0:T(8,128)}), (f32[3,256,128]{2,1,0:T(8,128)}, f32[128,256]{1,0:T(8,128)}, f32[3,256,128]{2,1,0:T(8,128)}, ...) | async-done | bytes 1048592 | tf_op jit(solution)/shard_map/psum | solution.py:53
  364.8 2.0 broadcast_multiply_fusion
  366.8 3.5 convolution_add_fusion.1
  370.4 4.6 %convolution_convert_fusion.4 = bf16[2048,60]{0,1:T(8,128)(2,1)S(1)} fusion(bf16[60,256]{1,0:T(8,128)(2,1)S(1)} %copy-done.28, f32[2048,256]{1,0:T(8,128)S(1)} %bitcast_add_fusion, f32[2048,256]{1,0:T(8,128)} %convolution_add_fusion.1, bf16[2048,128]{1,0:T(8,128)(2,1)} %collective-permute-done.9, f32[2048,256]{1,0:T(8,128)} %copy-done.29, ...), kind=kOutput, calls=%fused_computation.42 | convolution fusion | flops 210362368 | bytes 7159808 | tf_op jit(solution)/shard_map/dot_general | solution.py:152
  375.1 3.1 collective-permute-start.10
  380.3 2.4 collective-permute-done.11
  (111 shorter events, 23.0 us)
Async XLA Ops:
  7.2 70.1 %copy-start = (bf16[192,256]{1,0:T(8,128)(2,1)S(1)}, bf16[192,256]{1,0:T(8,128)(2,1)}, u32[]{:S(2)}) copy-start(bf16[192,256]{1,0:T(8,128)(2,1)} %param.14) | copy-start | bytes 294916
  7.2 8.0 %copy-start.27 = (bf16[60,256]{1,0:T(8,128)(2,1)S(1)}, bf16[60,256]{1,0:T(8,128)(2,1)}, u32[]{:S(2)}) copy-start(bf16[60,256]{1,0:T(8,128)(2,1)} %param.9) | copy-start | bytes 92164
  7.2 131.9 %reduce-scatter.2.cloned.1.call-start = ((), (), s32[]{:S(2)}) async-start(), calls=%async_computation.1 | async-start | bytes 147456 | tf_op jit(solution)/shard_map/reduce_scatter | solution.py:134
  8.0 6.0 %collective-permute-start.1 = (s32[7]{0:T(128)S(1)}, s32[7]{0:T(128)S(1)}, u32[]{:S(2)}, u32[]{:S(2)}) collective-permute-start(s32[7]{0:T(128)S(1)} %get-tuple-element.29), channel_id=1, source_target_pairs={{4,0},{8,4},{12,8},{16,12},{20,16},{24,20},{28,24},{5,1},{9,5},{13... | collective-permute-start | bytes 92 | tf_op jit(solution)/shard_map/ppermute | solution.py:26
  9.3 5.3 %collective-permute-start = (s32[7]{0:T(128)S(1)}, s32[7]{0:T(128)S(1)}, u32[]{:S(2)}, u32[]{:S(2)}) collective-permute-start(s32[7]{0:T(128)S(1)} %get-tuple-element.30), channel_id=1, source_target_pairs={{0,4},{4,8},{8,12},{12,16},{16,20},{20,24},{24,28},{1,5},{5,9},{9,... | collective-permute-start | bytes 92 | tf_op jit(solution)/shard_map/ppermute | solution.py:24
  15.2 6.7 %copy-start.15 = (bf16[3,256,128]{2,1,0:T(8,128)(2,1)S(1)}, bf16[3,256,128]{2,1,0:T(8,128)(2,1)}, u32[]{:S(2)}) copy-start(bf16[3,256,128]{2,1,0:T(8,128)(2,1)} %param.10) | copy-start | bytes 589828
  16.3 47.8 %copy-start.8 = (bf16[2048,256]{1,0:T(8,128)(2,1)}, bf16[2048,256]{1,0:T(8,128)(2,1)S(1)}, u32[]{:S(2)}) copy-start(bf16[2048,256]{1,0:T(8,128)(2,1)S(1)} %get-tuple-element.33) | copy-start | bytes 3145732
  16.3 48.8 %copy-start.29 = (f32[2048,256]{1,0:T(8,128)}, f32[2048,256]{1,0:T(8,128)S(1)}, u32[]{:S(2)}) copy-start(f32[2048,256]{1,0:T(8,128)S(1)} %get-tuple-element.34) | copy-start | bytes 6291460
  16.3 47.4 %collective-permute-start.2 = (bf16[2048,256]{1,0:T(8,128)(2,1)S(1)}, bf16[2048,256]{1,0:T(8,128)(2,1)S(1)}, u32[]{:S(2)}, u32[]{:S(2)}) collective-permute-start(bf16[2048,256]{1,0:T(8,128)(2,1)S(1)} %get-tuple-element.33), channel_id=1, source_target_pairs={{0,4},{4,8},{8,12},{12,16},{16,20},{20,24},{24,28},{1,5},{5,9},{9,... | collective-permute-start | bytes 3145736 | tf_op jit(solution)/shard_map/ppermute | solution.py:13
  20.6 43.5 %collective-permute-start.3 = (bf16[2048,256]{1,0:T(8,128)(2,1)S(1)}, bf16[2048,256]{1,0:T(8,128)(2,1)S(1)}, u32[]{:S(2)}, u32[]{:S(2)}) collective-permute-start(bf16[2048,256]{1,0:T(8,128)(2,1)S(1)} %get-tuple-element.33), channel_id=1, source_target_pairs={{4,0},{8,4},{12,8},{16,12},{20,16},{24,20},{28,24},{5,1},{9,5},{13... | collective-permute-start | bytes 3145736 | tf_op jit(solution)/shard_map/ppermute | solution.py:13
  65.1 126.5 %copy-start.1 = (f32[2048,128]{1,0:T(8,128)}, f32[2048,128]{1,0:T(8,128)S(1)}, u32[]{:S(2)}) copy-start(f32[2048,128]{1,0:T(8,128)S(1)} %fusion.14) | copy-start | bytes 3145732
  65.1 12.1 %copy-start.18 = (bf16[1,192,128]{2,1,0:T(8,128)(2,1)S(1)}, bf16[1,192,128]{2,1,0:T(8,128)(2,1)}, u32[]{:S(2)}) copy-start(bf16[1,192,128]{2,1,0:T(8,128)(2,1)} %param.15) | copy-start | bytes 147460
  65.1 13.0 %copy-start.14 = (bf16[3,256,128]{2,1,0:T(8,128)(2,1)S(1)}, bf16[3,256,128]{2,1,0:T(8,128)(2,1)}, u32[]{:S(2)}) copy-start(bf16[3,256,128]{2,1,0:T(8,128)(2,1)} %param.12) | copy-start | bytes 589828
  67.7 31.1 %collective-permute-start.4 = (bf16[2048,256]{1,0:T(8,128)(2,1)}, bf16[2048,256]{1,0:T(8,128)(2,1)S(1)}, u32[]{:S(2)}, u32[]{:S(2)}) collective-permute-start(bf16[2048,256]{1,0:T(8,128)(2,1)} %get-tuple-element.35), channel_id=1, source_target_pairs={{0,8},{4,12},{8,16},{12,20},{16,24},{20,28},{1,9},{5,13},{9,17},{1... | collective-permute-start | bytes 3145736 | tf_op jit(solution)/shard_map/ppermute | solution.py:13
  75.9 26.9 %collective-permute-start.5 = (bf16[2048,256]{1,0:T(8,128)(2,1)}, bf16[2048,256]{1,0:T(8,128)(2,1)S(1)}, u32[]{:S(2)}, u32[]{:S(2)}) collective-permute-start(bf16[2048,256]{1,0:T(8,128)(2,1)} %get-tuple-element.35), channel_id=1, source_target_pairs={{8,0},{12,4},{16,8},{20,12},{24,16},{28,20},{9,1},{13,5},{17,9},{2... | collective-permute-start | bytes 3145736 | tf_op jit(solution)/shard_map/ppermute | solution.py:13
  78.1 143.8 %all-reduce.4.cloned.1.call-start = ((), (), s32[]{:S(2)}) async-start(), calls=%async_computation.2 | async-start | bytes 393216 | tf_op jit(solution)/shard_map/psum | solution.py:142
  98.8 5.4 %copy-start.6 = (bf16[2048,256]{1,0:T(8,128)(2,1)}, bf16[2048,256]{1,0:T(8,128)(2,1)S(1)}, u32[]{:S(2)}) copy-start(bf16[2048,256]{1,0:T(8,128)(2,1)S(1)} %collective-permute-done.4) | copy-start | bytes 3145732
  99.2 5.8 %copy-start.12 = (bf16[2048,256]{1,0:T(8,128)(2,1)S(1)}, bf16[2048,256]{1,0:T(8,128)(2,1)}, u32[]{:S(2)}) copy-start(bf16[2048,256]{1,0:T(8,128)(2,1)} %get-tuple-element.36) | copy-start | bytes 3145732
  99.2 5.7 %copy-start.25 = (bf16[128,256]{1,0:T(8,128)(2,1)S(1)}, bf16[128,256]{1,0:T(8,128)(2,1)}, u32[]{:S(2)}) copy-start(bf16[128,256]{1,0:T(8,128)(2,1)} %param.13) | copy-start | bytes 196612
  105.0 37.1 %copy-start.11 = (f32[2048,128]{1,0:T(8,128)S(1)}, f32[2048,128]{1,0:T(8,128)}, u32[]{:S(2)}) copy-start(f32[2048,128]{1,0:T(8,128)} %get-tuple-element.38) | copy-start | bytes 3145732
  147.4 40.4 %collective-permute-start.6 = (bf16[2048,128]{1,0:T(8,128)(2,1)}, bf16[2048,128]{1,0:T(8,128)(2,1)}, u32[]{:S(2)}, u32[]{:S(2)}) collective-permute-start(bf16[2048,128]{1,0:T(8,128)(2,1)} %fusion.7), channel_id=1, source_target_pairs={{8,0},{12,4},{16,8},{20,12},{24,16},{28,20},{9,1},{13,5},{17,9},{2... | collective-permute-start | bytes 1572872 | tf_op jit(solution)/shard_map/ppermute | solution.py:13
  148.7 40.7 %collective-permute-start.7 = (bf16[2048,128]{1,0:T(8,128)(2,1)}, bf16[2048,128]{1,0:T(8,128)(2,1)}, u32[]{:S(2)}, u32[]{:S(2)}) collective-permute-start(bf16[2048,128]{1,0:T(8,128)(2,1)} %fusion.7), channel_id=1, source_target_pairs={{0,8},{4,12},{8,16},{12,20},{16,24},{20,28},{1,9},{5,13},{9,17},{1... | collective-permute-start | bytes 1572872 | tf_op jit(solution)/shard_map/ppermute | solution.py:13
  183.2 181.6 %all-reduce.6.cloned.1.call-start = ((), (), s32[]{:S(2)}) async-start(), calls=%async_computation.3 | async-start | bytes 2097152 | tf_op jit(solution)/shard_map/psum | solution.py:53
  183.2 3.7 copy-start.17
  195.9 33.9 %copy-start.16 = (bf16[3,256,128]{2,1,0:T(8,128)(2,1)S(1)}, bf16[3,256,128]{2,1,0:T(8,128)(2,1)}, u32[]{:S(2)}) copy-start(bf16[3,256,128]{2,1,0:T(8,128)(2,1)} %param.10) | copy-start | bytes 589828
  223.6 143.3 %collective-permute-start.8 = (bf16[2048,128]{1,0:T(8,128)(2,1)S(1)}, bf16[2048,128]{1,0:T(8,128)(2,1)}, u32[]{:S(2)}, u32[]{:S(2)}) collective-permute-start(bf16[2048,128]{1,0:T(8,128)(2,1)S(1)} %fusion.8), channel_id=1, source_target_pairs={{4,0},{8,4},{12,8},{16,12},{20,16},{24,20},{28,24},{5,1},{9,5},{13... | collective-permute-start | bytes 1572872 | tf_op jit(solution)/shard_map/ppermute | solution.py:13
  224.9 145.5 %collective-permute-start.9 = (bf16[2048,128]{1,0:T(8,128)(2,1)S(1)}, bf16[2048,128]{1,0:T(8,128)(2,1)}, u32[]{:S(2)}, u32[]{:S(2)}) collective-permute-start(bf16[2048,128]{1,0:T(8,128)(2,1)S(1)} %fusion.8), channel_id=1, source_target_pairs={{0,4},{4,8},{8,12},{12,16},{16,20},{20,24},{24,28},{1,5},{5,9},{9,... | collective-permute-start | bytes 1572872 | tf_op jit(solution)/shard_map/ppermute | solution.py:13
  366.8 3.6 copy-start.28
  370.4 9.2 %copy-start.21 = (f32[128,256]{1,0:T(8,128)S(1)}, f32[128,256]{1,0:T(8,128)}, u32[]{:S(2)}) copy-start(f32[128,256]{1,0:T(8,128)} %get-tuple-element.8) | copy-start | bytes 393220
  370.4 9.2 %copy-start.22 = (f32[128,256]{1,0:T(8,128)S(1)}, f32[128,256]{1,0:T(8,128)}, u32[]{:S(2)}) copy-start(f32[128,256]{1,0:T(8,128)} %get-tuple-element.10) | copy-start | bytes 393220
  375.1 5.2 %collective-permute-start.10 = (bf16[7,60]{0,1:T(8,128)(2,1)S(1)}, bf16[7,60]{0,1:T(8,128)(2,1)S(1)}, u32[]{:S(2)}, u32[]{:S(2)}) collective-permute-start(bf16[7,60]{0,1:T(8,128)(2,1)S(1)} %get-tuple-element.12), channel_id=1, source_target_pairs={{0,4},{4,8},{8,12},{12,16},{16,20},{20,24},{24,28},{1,5},{5,9},{9,... | collective-permute-start | bytes 2528 | tf_op jit(solution)/shard_map/ppermute | solution.py:24
  378.2 4.5 %collective-permute-start.11 = (bf16[7,60]{0,1:T(8,128)(2,1)S(1)}, bf16[7,60]{0,1:T(8,128)(2,1)S(1)}, u32[]{:S(2)}, u32[]{:S(2)}) collective-permute-start(bf16[7,60]{0,1:T(8,128)(2,1)S(1)} %get-tuple-element.11), channel_id=1, source_target_pairs={{4,0},{8,4},{12,8},{16,12},{20,16},{24,20},{28,24},{5,1},{9,5},{13... | collective-permute-start | bytes 2528 | tf_op jit(solution)/shard_map/ppermute | solution.py:26
  (13 other events, 22.8 us)
Sparse Core Ops, SparseCore 0:
  78.2 60.8 reduce-scatter.1
  183.3 38.6 all-reduce.3
  229.0 135.7 all-reduce.5
where the time goes:
time: 394 us; the launch traced here: 390 us
  waiting for transfers between devices  259 us (66%)
  matrix products  40.5 us (10%)
  starting transfers between devices  37.8 us (10%)
  blocking collectives  28 us (7%)
  between operations  14.3 us (4%)
  other arithmetic  8.53 us (2%)
    psum x1, waiting for transfers between devices, reduce_grads(): return lax.psum((conv_raw, proj_raw), ('seq', 'dp'))  133 us
    ppermute x8, waiting for transfers between devices, passed_along(): lax.ppermute(value, axis, [(source, source + steps) for source in range(f...  63.8 us
    reduce_scatter x1, waiting for transfers between devices, per_device(): lax.psum_scatter(lax.dot_general(cot_rows, bin_weight, (((0,), (0,)), (()...  33.7 us
    all_gather x1, blocking collectives, per_device(): gathered = lax.all_gather(pooled_act, 'seq', axis=0, tiled=True)  28 us
    ppermute x8, starting transfers between devices, passed_along(): lax.ppermute(value, axis, [(source, source + steps) for source in range(f...  27.4 us
    psum x1, waiting for transfers between devices, per_device(): bin_total = lax.psum(bin_part, 'dp')  24.8 us
  transfers between devices with their start and end apart: 15, of which 8 were waited for; matrix products, arithmetic and copies ran while one was open for 8% of the time, Pallas kernels for 0%

commit v1 on v0

--- a/solution.py
+++ b/solution.py
@@ -1,6 +1,10 @@
+import functools
+
 import jax
 import jax.numpy as jnp
 from jax import lax
+from jax.experimental import pallas as pl
+from jax.experimental.pallas import tpu as pltpu
 from jax.sharding import PartitionSpec as P
 
 STEM = 15
@@ -168,10 +172,519 @@
     )
 
 
+NN = (((1,), (0,)), ((), ()))
+NT = (((1,), (1,)), ((), ()))
+TN = (((0,), (0,)), ((), ()))
+F32 = jnp.float32
+BF16 = jnp.bfloat16
+WIRE = jnp.bfloat16
+
+
+def mm(left, right, dims=NN):
+    return lax.dot_general(left, right, dims, preferred_element_type=F32)
+
+
+def gelu_pair(value):
+    cdf = 0.5 + 0.5 * lax.erf(value * 0.7071067811865476)
+    slope = cdf + value * (jnp.exp(-0.5 * value * value) * 0.3989422804014327)
+    return value * cdf, slope
+
+
+def tower_kernel(
+    n_seq,
+    n_dp,
+    scale,
+    bases_ref,
+    stem_ref,
+    conv1_ref,
+    proj1_ref,
+    conv2_ref,
+    proj2_ref,
+    binw_ref,
+    cot_ref,
+    preds_ref,
+    sal_ref,
+    conv1_out,
+    proj1_out,
+    conv2_out,
+    proj2_out,
+    bin_out,
+    ids,
+    stem_pad,
+    slope_stem,
+    stream0,
+    act0,
+    slope0,
+    slope_pre1,
+    inner1,
+    stream1,
+    act1,
+    slope1,
+    slope_pre2,
+    pooled,
+    inner_sum,
+    bin_grad,
+    bin_inner,
+    pg2,
+    pg1,
+    grad1,
+    wcat,
+    part_out,
+    part_in,
+    pool_all,
+    bin_all,
+    conv_acc,
+    proj_acc,
+    rs_out,
+    rs_in,
+    rs2_out,
+    rs2_in,
+    ag,
+    ag_all,
+    sal_out,
+    sal_in,
+    send_sem,
+    recv_sem,
+):
+    seq = lax.axis_index("seq")
+    dp = lax.axis_index("dp")
+    length = bases_ref.shape[1]
+    width = stem_ref.shape[1]
+    hid = proj1_ref.shape[0]
+    seg = length // n_seq
+    per_seg = seg // POOL
+    n_bins = n_seq * per_seg
+    half = STEM // 2
+
+    barrier = pltpu.get_barrier_semaphore()
+    for i in range(1, n_seq):
+        pl.semaphore_signal(
+            barrier,
+            inc=1,
+            device_id=(lax.rem(seq + i, n_seq), dp),
+            device_id_type=pl.DeviceIdType.MESH,
+        )
+    for i in range(1, n_dp):
+        pl.semaphore_signal(
+            barrier,
+            inc=1,
+            device_id=(seq, lax.rem(dp + i, n_dp)),
+            device_id_type=pl.DeviceIdType.MESH,
+        )
+    used = [0]
+
+    def send(axis, source, target):
+        count = n_seq if axis == "seq" else n_dp
+        copies = []
+        for i in range(1, count):
+            if axis == "seq":
+                peer = lax.rem(seq + i, count)
+                where = (peer, dp)
+            else:
+                peer = lax.rem(dp + i, count)
+                where = (seq, peer)
+            slot = used[0]
+            used[0] += 1
+            copy = pltpu.make_async_remote_copy(
+                src_ref=source(peer),
+                dst_ref=target(i),
+                send_sem=send_sem.at[slot],
+                recv_sem=recv_sem.at[slot],
+                device_id=where,
+                device_id_type=pl.DeviceIdType.MESH,
+            )
+            copy.start()
+            copies.append(copy)
+        return copies
+
+    def finish(copies):
+        for copy in copies:
+            copy.wait()
+
+    def rows_of(chunk):
+        return pl.ds(pl.multiple_of(chunk * seg, seg), seg)
+
+    outside = jnp.full((1, 1, length), -1, jnp.int32)
+    ids[pl.ds(0, 1)] = outside
+    ids[pl.ds(n_seq + 1, 1)] = outside
+    ids[pl.ds(seq + 1, 1)] = bases_ref[...].reshape(1, 1, length)
+    pl.semaphore_wait(barrier, n_seq - 1 + n_dp - 1)
+    ids_copies = send("seq", lambda peer: ids.at[seq + 1], lambda i: ids.at[seq + 1])
+
+    bins_total = n_bins * n_seq
+    nat = lax.broadcasted_iota(jnp.int32, (bins_total, bins_total), 0)
+    got = lax.broadcasted_iota(jnp.int32, (bins_total, bins_total), 1)
+    h_bits = per_seg.bit_length() - 1
+    s_bits = n_seq.bit_length() - 1
+    chunk_of = nat >> (h_bits + s_bits)
+    owner_of = (nat >> h_bits) & (n_seq - 1)
+    place = (owner_of << (h_bits + s_bits)) | (chunk_of << h_bits) | (nat & (per_seg - 1))
+    perm = (place == got).astype(F32).astype(BF16)
+
+    cot = cot_ref[...].reshape(cot_ref.shape[1], cot_ref.shape[2])
+    cot_perm = mm(cot, perm).astype(BF16)
+    part_out[...] = mm(cot_perm, binw_ref[...], TN).reshape(n_seq, n_bins, width)
+    part_copies = send("seq", lambda peer: part_out.at[peer], lambda i: part_in.at[i - 1])
+
+    stem_pad[...] = jnp.concatenate(
+        [stem_ref[...].astype(F32), jnp.zeros((64 - 4 * STEM, width), F32)], axis=0
+    ).astype(BF16)
+    wcat[0] = jnp.concatenate([conv1_ref[0], conv1_ref[1], conv1_ref[2]], axis=1)
+    wcat[1] = jnp.concatenate([conv2_ref[0], conv2_ref[1], conv2_ref[2]], axis=1)
+    act0[pl.ds(0, seg)] = jnp.zeros((seg, width), BF16)
+    act0[pl.ds((n_seq + 1) * seg, seg)] = jnp.zeros((seg, width), BF16)
+    act1[pl.ds(0, 2 * seg)] = jnp.zeros((2 * seg, width), BF16)
+    act1[pl.ds((n_seq + 2) * seg, 2 * seg)] = jnp.zeros((2 * seg, width), BF16)
+    pg1[pl.ds(0, seg)] = jnp.zeros((seg, hid), BF16)
+    pg1[pl.ds((n_seq + 1) * seg, seg)] = jnp.zeros((seg, hid), BF16)
+    pg2[pl.ds(0, 2 * seg)] = jnp.zeros((2 * seg, hid), BF16)
+    pg2[pl.ds((n_seq + 2) * seg, 2 * seg)] = jnp.zeros((2 * seg, hid), BF16)
+    sal_out[...] = jnp.zeros_like(sal_out)
+    pooled[...] = jnp.zeros_like(pooled)
+    inner_sum[...] = jnp.zeros_like(inner_sum)
+
+    first = (seq == 0).astype(jnp.int32)
+    last = (seq == n_seq - 1).astype(jnp.int32)
+    low = pl.multiple_of(lax.rem(seq * seg + length - 128, length), 128)
+    high = pl.multiple_of(lax.rem(seq * seg + seg, length), 128)
+    span = seg + 256
+    finish(ids_copies)
+
+    def stem_chunk(chunk, carry):
+        line = jnp.concatenate(
+            [
+                ids[chunk + 1 - first, :, pl.ds(low, 128)],
+                ids[chunk + 1, :, pl.ds(pl.multiple_of(seq * seg, seg), seg)],
+                ids[chunk + 1 + last, :, pl.ds(high, 128)],
+            ],
+            axis=1,
+        )
+        block = jnp.broadcast_to(line, (8, span))
+        sub = lax.broadcasted_iota(jnp.int32, (8, span), 0)
+        block = jnp.where(sub < 4, block, pltpu.roll(block, span - 1, 1))
+        letter = (sub & 3)[:, :seg]
+        tiles = []
+        for m in range(8):
+            moved = pltpu.roll(block, span - (128 - half + 2 * m), 1)[:, :seg]
+            tiles.append((moved == letter).astype(F32))
+        codes = jnp.concatenate(tiles, axis=0).astype(BF16)
+        pre = mm(codes, stem_pad[...], TN)
+        value, slope = gelu_pair(pre)
+        rows = rows_of(chunk)
+        slope_stem[rows] = slope
+        value = value.astype(BF16)
+        stream0[rows] = value
+        act, slope = gelu_pair(value.astype(F32))
+        slope0[rows] = slope
+        act0[rows_of(chunk + 1)] = act.astype(BF16)
+        return carry
+
+    lax.fori_loop(0, n_seq, stem_chunk, 0)
+
+    def pre_of(act, conv_ref, chunk, hops):
+        wide = jnp.concatenate(
+            [act[rows_of(chunk)], act[rows_of(chunk + hops)], act[rows_of(chunk + 2 * hops)]],
+            axis=1,
+        )
+        return mm(wide, conv_ref[...].reshape(3 * width, hid))
+
+    def first_chunk(chunk, carry):
+        rows = rows_of(chunk)
+        inner, slope = gelu_pair(pre_of(act0, conv1_ref, chunk, 1))
+        slope_pre1[rows] = slope
+        inner = inner.astype(BF16)
+        inner1[rows] = inner
+        result = (stream0[rows].astype(F32) + mm(inner, proj1_ref[...])).astype(BF16)
+        stream1[rows] = result
+        act, slope = gelu_pair(result.astype(F32))
+        slope1[rows] = slope
+        act1[rows_of(chunk + 2)] = act.astype(BF16)
+        return carry
+
+    lax.fori_loop(0, n_seq, first_chunk, 0)
+
+    def second_chunk(chunk, carry):
+        rows = rows_of(chunk)
+        inner, slope = gelu_pair(pre_of(act1, conv2_ref, chunk, 2))
+        slope_pre2[rows] = slope
+        inner = inner.astype(BF16)
+        result = (stream1[rows].astype(F32) + mm(inner, proj2_ref[...])).astype(BF16)
+        bin_row = lax.broadcasted_iota(jnp.int32, (n_bins, seg), 0)
+        bin_pos = lax.broadcasted_iota(jnp.int32, (n_bins, seg), 1) // POOL
+        member = (bin_row == bin_pos + chunk * per_seg).astype(F32).astype(BF16)
+        pooled[...] += mm(member, result)
+        inner_sum[...] += mm(member, inner)
+        return carry
+
+    lax.fori_loop(0, n_seq, second_chunk, 0)
+
+    pooled_act, pooled_slope = gelu_pair(pooled[...] * (1.0 / POOL))
+    pool_all[pl.ds(seq, 1)] = pooled_act.astype(BF16).reshape(1, n_bins, width)
+    pool_copies = send("seq", lambda peer: pool_all.at[seq], lambda i: pool_all.at[seq])
+
+    finish(part_copies)
+    total = part_out[seq]
+    for i in range(n_seq - 1):
+        total = total + part_in[i]
+    grad2 = total * pooled_slope * (1.0 / POOL)
+    bin_grad[...] = grad2
+    grad2_in = grad2.astype(BF16)
+    bin_inner[...] = mm(grad2_in, proj2_ref[...], NT)
+
+    isum = inner_sum[...]
+    coarse = isum.astype(BF16)
+    fine = (isum - coarse.astype(F32)).astype(BF16)
+    proj_acc[...] = mm(coarse, grad2_in, TN) + mm(fine, grad2_in, TN)
+
+    def spread(ref, chunk, columns):
+        return jnp.concatenate(
+            [
+                jnp.broadcast_to(ref[pl.ds(chunk * per_seg + h, 1), :], (POOL, columns))
+                for h in range(per_seg)
+            ],
+            axis=0,
+        )
+
+    def grad2_chunk(chunk, carry):
+        wide = spread(bin_inner, chunk, hid)
+        pg2[rows_of(chunk + 2)] = (wide * slope_pre2[rows_of(chunk)]).astype(BF16)
+        return carry
+
+    lax.fori_loop(0, n_seq, grad2_chunk, 0)
+
+    def around(pg, chunk, hops):
+        return jnp.concatenate(
+            [pg[rows_of(chunk + 2 * hops)], pg[rows_of(chunk + hops)], pg[rows_of(chunk)]], axis=1
+        )
+
+    def conv_grads(act, pg, hops):
+        conv_acc[...] = jnp.zeros_like(conv_acc)
+
+        def step(chunk, carry):
+            conv_acc[...] += mm(act[rows_of(chunk + hops)], around(pg, chunk, hops), TN)
+            return carry
+
+        lax.fori_loop(0, n_seq, step, 0)
+
+    piece = width // n_seq
+
+    def reduce_one(b):
+        for t in range(3):
+            rs_out[b, t] = conv_acc[:, t * hid : (t + 1) * hid].astype(WIRE)
+        for t in range(width // hid):
+            rs_out[b, 3, pl.ds(t * hid, hid)] = proj_acc[:, t * hid : (t + 1) * hid].astype(WIRE)
+        return send("dp", lambda peer: rs_out.at[b, peer], lambda i: rs_in.at[b, i - 1])
+
+    def reduce_two(b, copies):
+        finish(copies)
+        total = rs_out[b, dp].astype(F32)
+        for i in range(n_dp - 1):
+            total = total + rs_in[b, i].astype(F32)
+        rs2_out[b] = total.reshape(n_seq, piece, hid)
+        return send("seq", lambda peer: rs2_out.at[b, peer], lambda i: rs2_in.at[b, i - 1])
+
+    def reduce_three(b, copies):
+        finish(copies)
+        total = rs2_out[b, seq]
+        for i in range(n_seq - 1):
+            total = total + rs2_in[b, i]
+        ag[b, pl.ds(seq, 1)] = (total * scale).astype(WIRE).reshape(1, piece, hid)
+        return send("seq", lambda peer: ag.at[b, seq], lambda i: ag.at[b, seq])
+
+    def reduce_four(b, copies):
+        finish(copies)
+        ag_all[b, pl.ds(dp, 1)] = ag[b].reshape(1, n_seq, piece, hid)
+        return send("dp", lambda peer: ag.at[b], lambda i: ag_all.at[b, dp])
+
+    def reduce_end(b, copies, conv_out, proj_out):
+        finish(copies)
+        for t in range(3):
+            conv_out[t] = ag_all[b, t].reshape(width, hid).astype(F32)
+        whole = ag_all[b, 3].reshape(width, hid).astype(F32)
+        for t in range(width // hid):
+            proj_out[:, t * hid : (t + 1) * hid] = whole[t * hid : (t + 1) * hid]
+
+    conv_grads(act1, pg2, 2)
+    two = reduce_one(0)
+
+    finish(pool_copies)
+    natural = mm(perm, pool_all[...].reshape(bins_total, width)).astype(BF16)
+    preds_ref[...] = mm(binw_ref[...], natural, NT).astype(BF16).reshape(preds_ref.shape)
+    bin_all[pl.ds(dp, 1)] = (
+        mm(cot, natural).astype(WIRE).reshape(1, binw_ref.shape[0], width)
+    )
+    bin_copies = send("dp", lambda peer: bin_all.at[dp], lambda i: bin_all.at[dp])
+
+    proj_acc[...] = jnp.zeros_like(proj_acc)
+
+    def grad1_chunk(chunk, carry):
+        rows = rows_of(chunk)
+        act_grad = mm(around(pg2, chunk, 2), wcat[1], NT)
+        grad = spread(bin_grad, chunk, width) + act_grad * slope1[rows]
+        grad1[rows] = grad
+        grad_in = grad.astype(BF16)
+        pg1[rows_of(chunk + 1)] = (mm(grad_in, proj1_ref[...], NT) * slope_pre1[rows]).astype(BF16)
+        proj_acc[...] += mm(inner1[rows], grad_in, TN)
+        return carry
+
+    lax.fori_loop(0, n_seq, grad1_chunk, 0)
+    two = reduce_two(0, two)
+    conv_grads(act0, pg1, 1)
+    one = reduce_one(1)
+    two = reduce_three(0, two)
+
+    wide_out = seg + 128
+
+    def saliency_chunk(chunk, carry):
+        rows = rows_of(chunk)
+        act_grad = mm(around(pg1, chunk, 1), wcat[0], NT)
+        grad = grad1[rows] + act_grad * slope0[rows]
+        stem_grad = (grad * slope_stem[rows]).astype(BF16)
+        code_grad = mm(stem_pad[...], stem_grad, NT)
+        code_grad = jnp.concatenate([code_grad, jnp.zeros((64, 128), F32)], axis=1)
+        total = jnp.zeros((8, wide_out), F32)
+        for m in range(8):
+            shift = (2 * m - half) % wide_out
+            tile = code_grad[8 * m : 8 * m + 8]
+            total = total + (pltpu.roll(tile, shift, 1) if shift else tile)
+        total = total[:4] + pltpu.roll(total, 1, 1)[4:]
+        sal_out[chunk + 1, pl.ds(0, 4)] = total
+        sal_out[chunk + 1 + jnp.where(seq == 0, -1, 1), pl.ds(4, 4)] = total
+        return carry
+
+    middle = n_seq // 2
+    lax.fori_loop(0, middle, saliency_chunk, 0)
+    one = reduce_two(1, one)
+    two = reduce_four(0, two)
+    lax.fori_loop(middle, n_seq, saliency_chunk, 0)
+    sal_in[pl.ds(seq, 1)] = sal_out[pl.ds(seq + 1, 1)]
+    sal_copies = send("seq", lambda peer: sal_out.at[peer + 1], lambda i: sal_in.at[seq])
+    one = reduce_three(1, one)
+
+    finish(bin_copies)
+    total = bin_all[0].astype(F32)
+    for d in range(1, n_dp):
+        total = total + bin_all[d].astype(F32)
+    bin_out[...] = total * scale
+    reduce_end(0, two, conv2_out, proj2_out)
+    one = reduce_four(1, one)
+
+    finish(sal_copies)
+    lane = lax.broadcasted_iota(jnp.int32, (4, 128), 1)
+
+    def rest(s, row):
+        return sal_in[s, row : row + 4, seg:]
+
+    for s in range(n_seq):
+        before = rest(s - 1, 0) if s > 0 else rest(n_seq - 1, 4)
+        after = rest(s + 1, 0) if s < n_seq - 1 else rest(0, 4)
+        block = sal_in[s, 0:4, 0:seg]
+        sal_ref[0, :, s * seg : s * seg + 128] = block[:, :128] + jnp.where(lane < 64, before, 0.0)
+        if seg > 256:
+            sal_ref[0, :, s * seg + 128 : (s + 1) * seg - 128] = block[:, 128 : seg - 128]
+        sal_ref[0, :, (s + 1) * seg - 128 : (s + 1) * seg] = block[:, seg - 128 :] + jnp.where(
+            lane >= 64, after, 0.0
+        )
+    reduce_end(1, one, conv1_out, proj1_out)
+
+
+def per_device_fused(
+    bases,
+    stem_table,
+    first_conv_taps,
+    first_projection_weight,
+    second_conv_taps,
+    second_projection_weight,
+    bin_weight,
+    cotangent,
+):
+    n_seq, n_dp = lax.axis_size("seq"), lax.axis_size("dp")
+    length = bases.shape[1]
+    width = stem_table.shape[1]
+    hid = first_projection_weight.shape[0]
+    seg = length // n_seq
+    n_bins = length // POOL
+    chans = bin_weight.shape[0]
+    scale = float(n_dp * n_seq * length) ** (-0.5)
+    copies = 5 * (n_seq - 1) + (n_dp - 1) + 2 * (2 * (n_seq - 1) + 2 * (n_dp - 1))
+    vmem = pl.BlockSpec(memory_space=pltpu.VMEM)
+    sds = jax.ShapeDtypeStruct
+    piece = width // n_seq
+    return pl.pallas_call(
+        functools.partial(tower_kernel, n_seq, n_dp, scale),
+        out_shape=(
+            sds((1, chans, cotangent.shape[2]), BF16),
+            sds((1, 4, length), F32),
+            sds((3, width, hid), F32),
+            sds((hid, width), F32),
+            sds((3, width, hid), F32),
+            sds((hid, width), F32),
+            sds((chans, width), F32),
+        ),
+        in_specs=[vmem] * 8,
+        out_specs=(vmem,) * 7,
+        scratch_shapes=[
+            pltpu.VMEM((n_seq + 2, 1, length), jnp.int32),
+            pltpu.VMEM((64, width), BF16),
+            pltpu.VMEM((length, width), F32),
+            pltpu.VMEM((length, width), BF16),
+            pltpu.VMEM((length + 2 * seg, width), BF16),
+            pltpu.VMEM((length, width), F32),
+            pltpu.VMEM((length, hid), F32),
+            pltpu.VMEM((length, hid), BF16),
+            pltpu.VMEM((length, width), BF16),
+            pltpu.VMEM((length + 4 * seg, width), BF16),
+            pltpu.VMEM((length, width), F32),
+            pltpu.VMEM((length, hid), F32),
+            pltpu.VMEM((n_bins, width), F32),
+            pltpu.VMEM((n_bins, hid), F32),
+            pltpu.VMEM((n_bins, width), F32),
+            pltpu.VMEM((n_bins, hid), F32),
+            pltpu.VMEM((length + 4 * seg, hid), BF16),
+            pltpu.VMEM((length + 2 * seg, hid), BF16),
+            pltpu.VMEM((length, width), F32),
+            pltpu.VMEM((2, width, 3 * hid), BF16),
+            pltpu.VMEM((n_seq, n_bins, width), F32),
+            pltpu.VMEM((n_seq - 1, n_bins, width), F32),
+            pltpu.VMEM((n_seq, n_bins, width), BF16),
+            pltpu.VMEM((n_dp, chans, width), WIRE),
+            pltpu.VMEM((width, 3 * hid), F32),
+            pltpu.VMEM((hid, width), F32),
+            pltpu.VMEM((2, n_dp, width, hid), WIRE),
+            pltpu.VMEM((2, n_dp - 1, width, hid), WIRE),
+            pltpu.VMEM((2, n_seq, piece, hid), F32),
+            pltpu.VMEM((2, n_seq - 1, piece, hid), F32),
+            pltpu.VMEM((2, n_seq, piece, hid), WIRE),
+            pltpu.VMEM((2, n_dp, n_seq, piece, hid), WIRE),
+            pltpu.VMEM((n_seq + 2, 8, seg + 128), F32),
+            pltpu.VMEM((n_seq, 8, seg + 128), F32),
+            pltpu.SemaphoreType.DMA((copies,)),
+            pltpu.SemaphoreType.DMA((copies,)),
+        ],
+        compiler_params=pltpu.CompilerParams(
+            collective_id=0, has_side_effects=True, vmem_limit_bytes=48 * 1024 * 1024
+        ),
+    )(
+        bases,
+        stem_table,
+        first_conv_taps,
+        first_projection_weight,
+        second_conv_taps,
+        second_projection_weight,
+        bin_weight,
+        cotangent,
+    )
+
+
+def fits_fused(mesh):
+    n_seq, n_dp = mesh.shape["seq"], mesh.shape["dp"]
+    return n_seq in (2, 4, 8) and n_dp == 4
+
+
 def solution(mesh):
     placed = (P("dp", "seq"), P(), P(), P(), P(), P(), P("seq", None), P("dp", "seq", None))
     return jax.shard_map(
-        per_device,
+        per_device_fused if fits_fused(mesh) else per_device,
         mesh=mesh,
         in_specs=placed,
         out_specs=(P("dp", "seq", None), P("dp", None, "seq"), P(), P(), P(), P(), P("seq", None)),

time: 394 us -> 65.7 us (0.17)
  waiting for transfers between devices: 259 us -> 0 us
  Pallas kernels: 0 us -> 53.2 us
  matrix products: 40.5 us -> 0 us
  starting transfers between devices: 37.8 us -> 0 us
  blocking collectives: 28 us -> 0 us
  between operations: 14.3 us -> 0.66 us
  local copies, waits for them, and re-layouts: 2.81 us -> 11.4 us
  other arithmetic: 8.53 us -> 0 us
    psum x2 -> x0, waiting for transfers between devices: 158 us -> none  [the longest x1 133 us: reduce_grads(): return lax.psum((conv_raw, proj_raw), ('seq', 'dp'))]
    ppermute x12 -> x0, waiting for transfers between devices: 66.7 us -> none  [the longest x8 63.8 us: passed_along(): lax.ppermute(value, axis, [(source, source + steps) for source in range(f...]
    pallas_call x0 -> x1, Pallas kernels: none -> 53.2 us  [per_device_fused(): pl.pallas_call(functools.partial(tower_kernel, n_seq, n_dp, scale), out_s...]
    dot_general x28 -> x0, matrix products: 40.5 us -> none  [the longest x2 5.1 us: residual_block_reverse(): jnp.dot(later, conv_w[0].T, preferred_element_type=jnp.float32)]
    ppermute x12 -> x0, starting transfers between devices: 37.7 us -> none  [the longest x8 27.4 us: passed_along(): lax.ppermute(value, axis, [(source, source + steps) for source in range(f...]
    reduce_scatter x1 -> x0, waiting for transfers between devices: 33.7 us -> none  [per_device(): lax.psum_scatter(lax.dot_general(cot_rows, bin_weight, (((0,), (0,)), (()...]
    all_gather x1 -> x0, blocking collectives: 28 us -> none  [per_device(): gathered = lax.all_gather(pooled_act, 'seq', axis=0, tiled=True)]
    unnamed x60 -> x23, local copies, waits for them, and re-layouts: 1.75 us -> 11.4 us
  transfers between devices with their start and end apart: 15 -> 0, of which waited for: 8 -> 0; matrix products, arithmetic and copies ran while one was open for 8% -> 0% of each run, Pallas kernels for 0% -> 0%
where the time goes in v1:
time: 65.7 us; the launch traced here: 65.3 us
  Pallas kernels  53.2 us (81%)
  local copies, waits for them, and re-layouts  11.4 us (17%)
  between operations  0.66 us (1%)
    pallas_call x1, Pallas kernels, per_device_fused(): pl.pallas_call(functools.partial(tower_kernel, n_seq, n_dp, scale), out_s...  53.2 us
    unnamed x23, local copies, waits for them, and re-layouts  11.4 us

profile of v1, /device:TPU:1, one launch (start us, length us, event | category | flops | bytes accessed | tf_op | source)
XLA Modules:
  0.0 65.3 jit_solution(12520353758766056874)
XLA Ops:
  0.6 0.0 copy-start
  0.6 0.9 %copy-done = bf16[3,256,128]{2,1,0:T(8,128)(2,1)S(1)} copy-done((bf16[3,256,128]{2,1,0:T(8,128)(2,1)S(1)}, bf16[3,256,128]{2,1,0:T(8,128)(2,1)}, u32[]{:S(2)}) %copy-start) | copy-done | bytes 196632
  1.6 0.0 copy-start.1
  1.6 0.9 %copy-done.1 = bf16[3,256,128]{2,1,0:T(8,128)(2,1)S(1)} copy-done((bf16[3,256,128]{2,1,0:T(8,128)(2,1)S(1)}, bf16[3,256,128]{2,1,0:T(8,128)(2,1)}, u32[]{:S(2)}) %copy-start.1) | copy-done | bytes 196632
  2.5 0.0 copy-start.2
  2.5 0.9 %copy-done.2 = bf16[192,256]{1,0:T(8,128)(2,1)S(1)} copy-done((bf16[192,256]{1,0:T(8,128)(2,1)S(1)}, bf16[192,256]{1,0:T(8,128)(2,1)}, u32[]{:S(2)}) %copy-start.2) | copy-done | bytes 98328
  3.4 0.0 copy-start.3
  3.4 0.8 %copy-done.3 = bf16[128,256]{1,0:T(8,128)(2,1)S(1)} copy-done((bf16[128,256]{1,0:T(8,128)(2,1)S(1)}, bf16[128,256]{1,0:T(8,128)(2,1)}, u32[]{:S(2)}) %copy-start.3) | copy-done | bytes 65560
  4.2 0.0 copy-start.4
  4.2 0.8 %copy-done.4 = bf16[128,256]{1,0:T(8,128)(2,1)S(1)} copy-done((bf16[128,256]{1,0:T(8,128)(2,1)S(1)}, bf16[128,256]{1,0:T(8,128)(2,1)}, u32[]{:S(2)}) %copy-start.4) | copy-done | bytes 65560
  5.1 0.0 copy-start.5
  5.1 0.8 %copy-done.5 = bf16[1,192,128]{2,1,0:T(8,128)(2,1)S(1)} copy-done((bf16[1,192,128]{2,1,0:T(8,128)(2,1)S(1)}, bf16[1,192,128]{2,1,0:T(8,128)(2,1)}, u32[]{:S(2)}) %copy-start.5) | copy-done | bytes 49176
  5.9 0.0 copy-start.6
  5.9 0.8 %copy-done.6 = bf16[60,256]{1,0:T(8,128)(2,1)S(1)} copy-done((bf16[60,256]{1,0:T(8,128)(2,1)S(1)}, bf16[60,256]{1,0:T(8,128)(2,1)}, u32[]{:S(2)}) %copy-start.6) | copy-done | bytes 30744
  6.6 0.0 copy-start.7
  6.6 0.7 %copy-done.7 = s32[1,2048]{1,0:T(1,128)S(1)} copy-done((s32[1,2048]{1,0:T(1,128)S(1)}, s32[1,2048]{1,0:T(1,128)}, u32[]{:S(2)}) %copy-start.7) | copy-done | bytes 8216
  7.3 53.2 %shard_map.135 = (bf16[1,192,128]{2,1,0:T(8,128)(2,1)S(1)}, f32[1,4,2048]{2,1,0:T(4,128)S(1)}, f32[3,256,128]{2,1,0:T(8,128)S(1)}, f32[128,256]{1,0:T(8,128)S(1)...) custom-call(s32[1,2048]{1,0:T(1,128)S(1)} %copy-done.7, ...), custom_call_target="tpu_custom_call" | custom-call | tf_op jit(solution)/shard_map/pallas_call | solution.py:613
  60.6 0.6 copy.22
  61.2 0.6 copy.23
  61.8 0.7 %copy.24 = f32[3,256,128]{2,1,0:T(8,128)} copy(f32[3,256,128]{2,1,0:T(8,128)S(1)} %get-tuple-element.16) | data formatting | bytes 786432
  62.6 0.7 %copy.25 = f32[128,256]{1,0:T(8,128)} copy(f32[128,256]{1,0:T(8,128)S(1)} %get-tuple-element.17) | data formatting | bytes 262144
  63.2 0.7 %copy.26 = f32[3,256,128]{2,1,0:T(8,128)} copy(f32[3,256,128]{2,1,0:T(8,128)S(1)} %get-tuple-element.18) | data formatting | bytes 786432
  64.0 0.7 %copy.27 = f32[128,256]{1,0:T(8,128)} copy(f32[128,256]{1,0:T(8,128)S(1)} %get-tuple-element.19) | data formatting | bytes 262144
  64.6 0.7 %copy.28 = f32[192,256]{1,0:T(8,128)} copy(f32[192,256]{1,0:T(8,128)S(1)} %get-tuple-element.20) | data formatting | bytes 393216
Async XLA Ops:
  0.6 0.9 %copy-start = (bf16[3,256,128]{2,1,0:T(8,128)(2,1)S(1)}, bf16[3,256,128]{2,1,0:T(8,128)(2,1)}, u32[]{:S(2)}) copy-start(bf16[3,256,128]{2,1,0:T(8,128)(2,1)} %conv1_ref.1) | copy-start | bytes 589828
  1.6 0.9 %copy-start.1 = (bf16[3,256,128]{2,1,0:T(8,128)(2,1)S(1)}, bf16[3,256,128]{2,1,0:T(8,128)(2,1)}, u32[]{:S(2)}) copy-start(bf16[3,256,128]{2,1,0:T(8,128)(2,1)} %conv2_ref.1) | copy-start | bytes 589828
  2.5 0.9 %copy-start.2 = (bf16[192,256]{1,0:T(8,128)(2,1)S(1)}, bf16[192,256]{1,0:T(8,128)(2,1)}, u32[]{:S(2)}) copy-start(bf16[192,256]{1,0:T(8,128)(2,1)} %binw_ref.1) | copy-start | bytes 294916
  3.4 0.8 %copy-start.3 = (bf16[128,256]{1,0:T(8,128)(2,1)S(1)}, bf16[128,256]{1,0:T(8,128)(2,1)}, u32[]{:S(2)}) copy-start(bf16[128,256]{1,0:T(8,128)(2,1)} %proj1_ref.1) | copy-start | bytes 196612
  4.2 0.8 %copy-start.4 = (bf16[128,256]{1,0:T(8,128)(2,1)S(1)}, bf16[128,256]{1,0:T(8,128)(2,1)}, u32[]{:S(2)}) copy-start(bf16[128,256]{1,0:T(8,128)(2,1)} %proj2_ref.1) | copy-start | bytes 196612
  5.1 0.8 %copy-start.5 = (bf16[1,192,128]{2,1,0:T(8,128)(2,1)S(1)}, bf16[1,192,128]{2,1,0:T(8,128)(2,1)}, u32[]{:S(2)}) copy-start(bf16[1,192,128]{2,1,0:T(8,128)(2,1)} %cot_ref.1) | copy-start | bytes 147460
  5.9 0.8 %copy-start.6 = (bf16[60,256]{1,0:T(8,128)(2,1)S(1)}, bf16[60,256]{1,0:T(8,128)(2,1)}, u32[]{:S(2)}) copy-start(bf16[60,256]{1,0:T(8,128)(2,1)} %stem_ref.1) | copy-start | bytes 92164
  6.6 0.7 %copy-start.7 = (s32[1,2048]{1,0:T(1,128)S(1)}, s32[1,2048]{1,0:T(1,128)}, u32[]{:S(2)}) copy-start(s32[1,2048]{1,0:T(1,128)} %bases_ref.1) | copy-start | bytes 24580

commit v2 on v1

--- a/solution.py
+++ b/solution.py
@@ -178,6 +178,7 @@
 F32 = jnp.float32
 BF16 = jnp.bfloat16
 WIRE = jnp.bfloat16
+KERNEL_VMEM = 57 * 1024 * 1024
 
 
 def mm(left, right, dims=NN):
@@ -185,8 +186,14 @@
 
 
 def gelu_pair(value):
-    cdf = 0.5 + 0.5 * lax.erf(value * 0.7071067811865476)
-    slope = cdf + value * (jnp.exp(-0.5 * value * value) * 0.3989422804014327)
+    t = 1.0 / (1.0 + 0.23164188825 * jnp.abs(value))
+    bell = jnp.exp2(value * value * -0.7213475204444817)
+    tail = 0.5307027145 * t - 0.7265760135
+    tail = tail * t + 0.7107068705
+    tail = tail * t - 0.142248368
+    tail = (tail * t + 0.127414796) * t * bell
+    cdf = jnp.where(value >= 0.0, 1.0 - tail, tail)
+    slope = cdf + value * (bell * 0.3989422804014327)
     return value * cdf, slope
 
 
@@ -194,6 +201,22 @@
     n_seq,
     n_dp,
     scale,
+    bases_in,
+    stem_in,
+    conv1_in,
+    proj1_in,
+    conv2_in,
+    proj2_in,
+    binw_in,
+    cot_in,
+    preds_out,
+    sal_final,
+    bin_final,
+    ag_final,
+    preds_ref,
+    sal_ref,
+    bin_out,
+    store_sem,
     bases_ref,
     stem_ref,
     conv1_ref,
@@ -202,14 +225,7 @@
     proj2_ref,
     binw_ref,
     cot_ref,
-    preds_ref,
-    sal_ref,
-    conv1_out,
-    proj1_out,
-    conv2_out,
-    proj2_out,
-    bin_out,
-    ids,
+    load_sem,
     stem_pad,
     slope_stem,
     stream0,
@@ -232,23 +248,41 @@
     part_out,
     part_in,
     pool_all,
-    bin_all,
     conv_acc,
     proj_acc,
-    rs_out,
-    rs_in,
+    two_out,
+    two_in,
+    one_out,
+    one_in,
     rs2_out,
     rs2_in,
-    ag,
+    fin_out,
+    fin_in,
     ag_all,
     sal_out,
-    sal_in,
     send_sem,
     recv_sem,
 ):
     seq = lax.axis_index("seq")
     dp = lax.axis_index("dp")
-    length = bases_ref.shape[1]
+    loads = [
+        pltpu.make_async_copy(source, target, load_sem.at[i])
+        for i, (source, target) in enumerate(
+            (
+                (bases_in, bases_ref),
+                (cot_in, cot_ref),
+                (binw_in, binw_ref),
+                (stem_in, stem_ref),
+                (conv1_in, conv1_ref),
+                (proj1_in, proj1_ref),
+                (conv2_in, conv2_ref),
+                (proj2_in, proj2_ref),
+            )
+        )
+    ]
+    for load in loads:
+        load.start()
+    length = bases_in.shape[1]
     width = stem_ref.shape[1]
     hid = proj1_ref.shape[0]
     seg = length // n_seq
@@ -304,13 +338,6 @@
     def rows_of(chunk):
         return pl.ds(pl.multiple_of(chunk * seg, seg), seg)
 
-    outside = jnp.full((1, 1, length), -1, jnp.int32)
-    ids[pl.ds(0, 1)] = outside
-    ids[pl.ds(n_seq + 1, 1)] = outside
-    ids[pl.ds(seq + 1, 1)] = bases_ref[...].reshape(1, 1, length)
-    pl.semaphore_wait(barrier, n_seq - 1 + n_dp - 1)
-    ids_copies = send("seq", lambda peer: ids.at[seq + 1], lambda i: ids.at[seq + 1])
-
     bins_total = n_bins * n_seq
     nat = lax.broadcasted_iota(jnp.int32, (bins_total, bins_total), 0)
     got = lax.broadcasted_iota(jnp.int32, (bins_total, bins_total), 1)
@@ -321,10 +348,22 @@
     place = (owner_of << (h_bits + s_bits)) | (chunk_of << h_bits) | (nat & (per_seg - 1))
     perm = (place == got).astype(F32).astype(BF16)
 
+    for load in loads:
+        load.wait()
     cot = cot_ref[...].reshape(cot_ref.shape[1], cot_ref.shape[2])
     cot_perm = mm(cot, perm).astype(BF16)
-    part_out[...] = mm(cot_perm, binw_ref[...], TN).reshape(n_seq, n_bins, width)
-    part_copies = send("seq", lambda peer: part_out.at[peer], lambda i: part_in.at[i - 1])
+    part = mm(cot_perm, binw_ref[...], TN).reshape(n_seq, n_bins, width)
+    ids = bases_ref[...].astype(F32)
+    ids = jnp.concatenate([ids[:, i * seg : (i + 1) * seg] for i in range(n_seq)], axis=0)
+    for i in range(n_seq):
+        part_out[i, :n_bins] = part[i]
+        part_out[i, n_bins:] = ids
+    outside = jnp.full((1, n_seq, width), -1.0, F32)
+    part_in[pl.ds(0, 1), n_bins:] = outside
+    part_in[pl.ds(n_seq + 1, 1), n_bins:] = outside
+    part_in[pl.ds(seq + 1, 1)] = part_out[pl.ds(seq, 1)]
+    pl.semaphore_wait(barrier, n_seq - 1 + n_dp - 1)
+    part_copies = send("seq", lambda peer: part_out.at[peer], lambda i: part_in.at[seq + 1])
 
     stem_pad[...] = jnp.concatenate(
         [stem_ref[...].astype(F32), jnp.zeros((64 - 4 * STEM, width), F32)], axis=0
@@ -345,24 +384,30 @@
 
     first = (seq == 0).astype(jnp.int32)
     last = (seq == n_seq - 1).astype(jnp.int32)
-    low = pl.multiple_of(lax.rem(seq * seg + length - 128, length), 128)
-    high = pl.multiple_of(lax.rem(seq * seg + seg, length), 128)
+    row_before = lax.rem(seq + n_seq - 1, n_seq)
+    row_after = lax.rem(seq + 1, n_seq)
+    row_index = lax.broadcasted_iota(jnp.int32, (n_seq, seg), 0)
+
+    def bases_row(slot, row):
+        picked = jnp.where(row_index == row, part_in[slot, n_bins:], 0.0)
+        return jnp.sum(picked, axis=0, keepdims=True)
+
     span = seg + 256
-    finish(ids_copies)
+    finish(part_copies)
 
     def stem_chunk(chunk, carry):
         line = jnp.concatenate(
             [
-                ids[chunk + 1 - first, :, pl.ds(low, 128)],
-                ids[chunk + 1, :, pl.ds(pl.multiple_of(seq * seg, seg), seg)],
-                ids[chunk + 1 + last, :, pl.ds(high, 128)],
+                bases_row(chunk + 1 - first, row_before)[:, seg - 128 :],
+                bases_row(chunk + 1, seq),
+                bases_row(chunk + 1 + last, row_after)[:, :128],
             ],
             axis=1,
         )
         block = jnp.broadcast_to(line, (8, span))
         sub = lax.broadcasted_iota(jnp.int32, (8, span), 0)
         block = jnp.where(sub < 4, block, pltpu.roll(block, span - 1, 1))
-        letter = (sub & 3)[:, :seg]
+        letter = (sub & 3)[:, :seg].astype(F32)
         tiles = []
         for m in range(8):
             moved = pltpu.roll(block, span - (128 - half + 2 * m), 1)[:, :seg]
@@ -422,10 +467,9 @@
     pool_all[pl.ds(seq, 1)] = pooled_act.astype(BF16).reshape(1, n_bins, width)
     pool_copies = send("seq", lambda peer: pool_all.at[seq], lambda i: pool_all.at[seq])
 
-    finish(part_copies)
-    total = part_out[seq]
-    for i in range(n_seq - 1):
-        total = total + part_in[i]
+    total = part_in[1, :n_bins]
+    for i in range(1, n_seq):
+        total = total + part_in[i + 1, :n_bins]
     grad2 = total * pooled_slope * (1.0 / POOL)
     bin_grad[...] = grad2
     grad2_in = grad2.astype(BF16)
@@ -467,53 +511,33 @@
         lax.fori_loop(0, n_seq, step, 0)
 
     piece = width // n_seq
-
-    def reduce_one(b):
+    n_chan = binw_ref.shape[0]
+
+    def put_parts(target):
         for t in range(3):
-            rs_out[b, t] = conv_acc[:, t * hid : (t + 1) * hid].astype(WIRE)
+            target[t, :width] = conv_acc[:, t * hid : (t + 1) * hid].astype(WIRE)
         for t in range(width // hid):
-            rs_out[b, 3, pl.ds(t * hid, hid)] = proj_acc[:, t * hid : (t + 1) * hid].astype(WIRE)
-        return send("dp", lambda peer: rs_out.at[b, peer], lambda i: rs_in.at[b, i - 1])
-
-    def reduce_two(b, copies):
-        finish(copies)
-        total = rs_out[b, dp].astype(F32)
-        for i in range(n_dp - 1):
-            total = total + rs_in[b, i].astype(F32)
-        rs2_out[b] = total.reshape(n_seq, piece, hid)
-        return send("seq", lambda peer: rs2_out.at[b, peer], lambda i: rs2_in.at[b, i - 1])
-
-    def reduce_three(b, copies):
-        finish(copies)
-        total = rs2_out[b, seq]
-        for i in range(n_seq - 1):
-            total = total + rs2_in[b, i]
-        ag[b, pl.ds(seq, 1)] = (total * scale).astype(WIRE).reshape(1, piece, hid)
-        return send("seq", lambda peer: ag.at[b, seq], lambda i: ag.at[b, seq])
-
-    def reduce_four(b, copies):
-        finish(copies)
-        ag_all[b, pl.ds(dp, 1)] = ag[b].reshape(1, n_seq, piece, hid)
-        return send("dp", lambda peer: ag.at[b], lambda i: ag_all.at[b, dp])
-
-    def reduce_end(b, copies, conv_out, proj_out):
-        finish(copies)
-        for t in range(3):
-            conv_out[t] = ag_all[b, t].reshape(width, hid).astype(F32)
-        whole = ag_all[b, 3].reshape(width, hid).astype(F32)
-        for t in range(width // hid):
-            proj_out[:, t * hid : (t + 1) * hid] = whole[t * hid : (t + 1) * hid]
+            target[3, t * hid : (t + 1) * hid] = proj_acc[:, t * hid : (t + 1) * hid].astype(WIRE)
 
     conv_grads(act1, pg2, 2)
-    two = reduce_one(0)
+    put_parts(two_out)
+    two = send("dp", lambda peer: two_out.at[peer], lambda i: two_in.at[i - 1])
 
     finish(pool_copies)
     natural = mm(perm, pool_all[...].reshape(bins_total, width)).astype(BF16)
     preds_ref[...] = mm(binw_ref[...], natural, NT).astype(BF16).reshape(preds_ref.shape)
-    bin_all[pl.ds(dp, 1)] = (
-        mm(cot, natural).astype(WIRE).reshape(1, binw_ref.shape[0], width)
-    )
-    bin_copies = send("dp", lambda peer: bin_all.at[dp], lambda i: bin_all.at[dp])
+    bin_raw = mm(cot, natural).astype(WIRE)
+    for d in range(n_dp):
+        for t in range(width // hid):
+            start = width + t * n_chan
+            one_out[d, start : start + n_chan] = bin_raw[:, t * hid : (t + 1) * hid]
+    stores = [
+        pltpu.make_async_copy(preds_ref, preds_out, store_sem.at[0]),
+        pltpu.make_async_copy(bin_out, bin_final, store_sem.at[1]),
+        pltpu.make_async_copy(sal_ref, sal_final, store_sem.at[2]),
+        pltpu.make_async_copy(ag_all, ag_final, store_sem.at[3]),
+    ]
+    stores[0].start()
 
     proj_acc[...] = jnp.zeros_like(proj_acc)
 
@@ -528,10 +552,10 @@
         return carry
 
     lax.fori_loop(0, n_seq, grad1_chunk, 0)
-    two = reduce_two(0, two)
     conv_grads(act0, pg1, 1)
-    one = reduce_one(1)
-    two = reduce_three(0, two)
+    put_parts(one_out)
+    one_in[pl.ds(dp, 1)] = one_out[pl.ds(dp, 1)]
+    one = send("dp", lambda peer: one_out.at[peer], lambda i: one_in.at[dp])
 
     wide_out = seg + 128
 
@@ -554,38 +578,102 @@
 
     middle = n_seq // 2
     lax.fori_loop(0, middle, saliency_chunk, 0)
-    one = reduce_two(1, one)
-    two = reduce_four(0, two)
+    finish(two)
+    total = two_out[dp].astype(F32)
+    for i in range(n_dp - 1):
+        total = total + two_in[i].astype(F32)
+    rs2_out[:, 0] = total.reshape(n_seq, piece, hid)
+    finish(one)
+    total = one_in[0, :width].astype(F32)
+    for d in range(1, n_dp):
+        total = total + one_in[d, :width].astype(F32)
+    rs2_out[:, 1] = total.reshape(n_seq, piece, hid)
+    summed = send("seq", lambda peer: rs2_out.at[peer], lambda i: rs2_in.at[i - 1])
     lax.fori_loop(middle, n_seq, saliency_chunk, 0)
-    sal_in[pl.ds(seq, 1)] = sal_out[pl.ds(seq + 1, 1)]
-    sal_copies = send("seq", lambda peer: sal_out.at[peer + 1], lambda i: sal_in.at[seq])
-    one = reduce_three(1, one)
-
-    finish(bin_copies)
-    total = bin_all[0].astype(F32)
-    for d in range(1, n_dp):
-        total = total + bin_all[d].astype(F32)
-    bin_out[...] = total * scale
-    reduce_end(0, two, conv2_out, proj2_out)
-    one = reduce_four(1, one)
-
-    finish(sal_copies)
+    blank = jnp.zeros((8, 128), F32)
+    for i in range(n_seq):
+        cells = sal_out[i + 1]
+        fin_out[i, 2 * piece :] = jnp.concatenate(
+            [cells[:, :128], cells[:, 128:256], cells[:, 256:], blank], axis=0
+        ).astype(WIRE)
+    finish(summed)
+    total = rs2_out[seq]
+    for i in range(n_seq - 1):
+        total = total + rs2_in[i]
+    total = (total * scale).astype(WIRE).reshape(2 * piece, hid)
+    for i in range(n_seq):
+        fin_out[i, : 2 * piece] = total
+    fin_in[pl.ds(seq, 1)] = fin_out[pl.ds(seq, 1)]
+    last_copies = send("seq", lambda peer: fin_out.at[peer], lambda i: fin_in.at[seq])
+
+    for t in range(width // hid):
+        start = width + t * n_chan
+        total = one_in[0, start : start + n_chan].astype(F32)
+        for d in range(1, n_dp):
+            total = total + one_in[d, start : start + n_chan].astype(F32)
+        bin_out[:, t * hid : (t + 1) * hid] = total * scale
+    stores[1].start()
+
+    finish(last_copies)
+    gathered = fin_in.at[:, pl.ds(0, 2 * piece)]
+    ag_copies = send("dp", lambda peer: gathered, lambda i: ag_all.at[dp])
+    ag_all[pl.ds(dp, 1)] = fin_in[:, : 2 * piece].reshape(1, n_seq, 2 * piece, hid)
+
     lane = lax.broadcasted_iota(jnp.int32, (4, 128), 1)
 
+    spots = [fin_in[s, 2 * piece :].astype(F32) for s in range(n_seq)]
+
     def rest(s, row):
-        return sal_in[s, row : row + 4, seg:]
+        return spots[s][16 + row : 20 + row]
 
     for s in range(n_seq):
         before = rest(s - 1, 0) if s > 0 else rest(n_seq - 1, 4)
         after = rest(s + 1, 0) if s < n_seq - 1 else rest(0, 4)
-        block = sal_in[s, 0:4, 0:seg]
-        sal_ref[0, :, s * seg : s * seg + 128] = block[:, :128] + jnp.where(lane < 64, before, 0.0)
-        if seg > 256:
-            sal_ref[0, :, s * seg + 128 : (s + 1) * seg - 128] = block[:, 128 : seg - 128]
-        sal_ref[0, :, (s + 1) * seg - 128 : (s + 1) * seg] = block[:, seg - 128 :] + jnp.where(
+        sal_ref[0, :, s * seg : s * seg + 128] = spots[s][0:4] + jnp.where(lane < 64, before, 0.0)
+        sal_ref[0, :, s * seg + 128 : (s + 1) * seg] = spots[s][8:12] + jnp.where(
             lane >= 64, after, 0.0
         )
-    reduce_end(1, one, conv1_out, proj1_out)
+    stores[2].start()
+    finish(ag_copies)
+    stores[3].start()
+    for store in stores:
+        store.wait()
+
+
+def store_kernel(*refs):
+    preds_in, sal_in, bin_in, ag_in = refs[:4]
+    outs = refs[4:11]
+    preds, sal, bins, ag, conv1, proj1, conv2, proj2, load_sem, store_sem = refs[11:]
+    loads = [
+        pltpu.make_async_copy(source, target, load_sem.at[i])
+        for i, (source, target) in enumerate(
+            ((ag_in, ag), (preds_in, preds), (sal_in, sal), (bin_in, bins))
+        )
+    ]
+    for load in loads:
+        load.start()
+    stores = [
+        pltpu.make_async_copy(source, target, store_sem.at[i])
+        for i, (source, target) in enumerate(
+            zip((preds, sal, conv1, proj1, conv2, proj2, bins), outs)
+        )
+    ]
+    hid, width = proj1.shape
+    piece = ag.shape[2] // 2
+    loads[0].wait()
+    for b, conv, proj, slot in ((0, conv2, proj2, 4), (1, conv1, proj1, 2)):
+        for t in range(3):
+            conv[t] = ag[t, :, b * piece : (b + 1) * piece].reshape(width, hid).astype(F32)
+        stores[slot].start()
+        whole = ag[3, :, b * piece : (b + 1) * piece].reshape(width, hid).astype(F32)
+        for t in range(width // hid):
+            proj[:, t * hid : (t + 1) * hid] = whole[t * hid : (t + 1) * hid]
+        stores[slot + 1].start()
+    for load, slot in zip(loads[1:], (0, 1, 6)):
+        load.wait()
+        stores[slot].start()
+    for store in stores:
+        store.wait()
 
 
 def per_device_fused(
@@ -606,25 +694,41 @@
     n_bins = length // POOL
     chans = bin_weight.shape[0]
     scale = float(n_dp * n_seq * length) ** (-0.5)
-    copies = 5 * (n_seq - 1) + (n_dp - 1) + 2 * (2 * (n_seq - 1) + 2 * (n_dp - 1))
-    vmem = pl.BlockSpec(memory_space=pltpu.VMEM)
+    copies = 4 * (n_seq - 1) + 3 * (n_dp - 1)
+    rows = width + 2 * chans
+    hbm = pl.BlockSpec(memory_space=pl.ANY)
     sds = jax.ShapeDtypeStruct
     piece = width // n_seq
-    return pl.pallas_call(
+    preds_shape = sds((1, chans, cotangent.shape[2]), BF16)
+    sal_shape = sds((1, 4, length), F32)
+    bin_shape = sds((chans, width), F32)
+    conv_shape = sds((3, width, hid), F32)
+    proj_shape = sds((hid, width), F32)
+    room = lambda leaf: pltpu.VMEM(leaf.shape, leaf.dtype)
+    made = pl.pallas_call(
         functools.partial(tower_kernel, n_seq, n_dp, scale),
         out_shape=(
-            sds((1, chans, cotangent.shape[2]), BF16),
-            sds((1, 4, length), F32),
-            sds((3, width, hid), F32),
-            sds((hid, width), F32),
-            sds((3, width, hid), F32),
-            sds((hid, width), F32),
-            sds((chans, width), F32),
+            preds_shape,
+            sal_shape,
+            bin_shape,
+            sds((n_dp, n_seq, 2 * piece, hid), WIRE),
         ),
-        in_specs=[vmem] * 8,
-        out_specs=(vmem,) * 7,
+        in_specs=[hbm] * 8,
+        out_specs=(hbm,) * 4,
         scratch_shapes=[
-            pltpu.VMEM((n_seq + 2, 1, length), jnp.int32),
+            room(preds_shape),
+            room(sal_shape),
+            room(bin_shape),
+            pltpu.SemaphoreType.DMA((4,)),
+            pltpu.VMEM((1, length), jnp.int32),
+            pltpu.VMEM(stem_table.shape, BF16),
+            pltpu.VMEM(first_conv_taps.shape, BF16),
+            pltpu.VMEM(first_projection_weight.shape, BF16),
+            pltpu.VMEM(second_conv_taps.shape, BF16),
+            pltpu.VMEM(second_projection_weight.shape, BF16),
+            pltpu.VMEM(bin_weight.shape, BF16),
+            pltpu.VMEM(cotangent.shape, BF16),
+            pltpu.SemaphoreType.DMA((8,)),
             pltpu.VMEM((64, width), BF16),
             pltpu.VMEM((length, width), F32),
             pltpu.VMEM((length, width), BF16),
@@ -644,25 +748,26 @@
             pltpu.VMEM((length + 2 * seg, hid), BF16),
             pltpu.VMEM((length, width), F32),
             pltpu.VMEM((2, width, 3 * hid), BF16),
-            pltpu.VMEM((n_seq, n_bins, width), F32),
-            pltpu.VMEM((n_seq - 1, n_bins, width), F32),
+            pltpu.VMEM((n_seq, n_bins + n_seq, width), F32),
+            pltpu.VMEM((n_seq + 2, n_bins + n_seq, width), F32),
             pltpu.VMEM((n_seq, n_bins, width), BF16),
-            pltpu.VMEM((n_dp, chans, width), WIRE),
             pltpu.VMEM((width, 3 * hid), F32),
             pltpu.VMEM((hid, width), F32),
-            pltpu.VMEM((2, n_dp, width, hid), WIRE),
-            pltpu.VMEM((2, n_dp - 1, width, hid), WIRE),
-            pltpu.VMEM((2, n_seq, piece, hid), F32),
-            pltpu.VMEM((2, n_seq - 1, piece, hid), F32),
-            pltpu.VMEM((2, n_seq, piece, hid), WIRE),
-            pltpu.VMEM((2, n_dp, n_seq, piece, hid), WIRE),
+            pltpu.VMEM((n_dp, width, hid), WIRE),
+            pltpu.VMEM((n_dp - 1, width, hid), WIRE),
+            pltpu.VMEM((n_dp, rows, hid), WIRE),
+            pltpu.VMEM((n_dp, rows, hid), WIRE),
+            pltpu.VMEM((n_seq, 2, piece, hid), F32),
+            pltpu.VMEM((n_seq - 1, 2, piece, hid), F32),
+            pltpu.VMEM((n_seq, 2 * piece + 32, hid), WIRE),
+            pltpu.VMEM((n_seq, 2 * piece + 32, hid), WIRE),
+            pltpu.VMEM((n_dp, n_seq, 2 * piece, hid), WIRE),
             pltpu.VMEM((n_seq + 2, 8, seg + 128), F32),
-            pltpu.VMEM((n_seq, 8, seg + 128), F32),
             pltpu.SemaphoreType.DMA((copies,)),
             pltpu.SemaphoreType.DMA((copies,)),
         ],
         compiler_params=pltpu.CompilerParams(
-            collective_id=0, has_side_effects=True, vmem_limit_bytes=48 * 1024 * 1024
+            collective_id=0, has_side_effects=True, vmem_limit_bytes=KERNEL_VMEM
         ),
     )(
         bases,
@@ -674,11 +779,31 @@
         bin_weight,
         cotangent,
     )
+    shapes = (preds_shape, sal_shape, conv_shape, proj_shape, conv_shape, proj_shape, bin_shape)
+    return pl.pallas_call(
+        store_kernel,
+        out_shape=shapes,
+        in_specs=[hbm] * 4,
+        out_specs=(hbm,) * 7,
+        scratch_shapes=[
+            room(preds_shape),
+            room(sal_shape),
+            room(bin_shape),
+            room(made[3]),
+            room(conv_shape),
+            room(proj_shape),
+            room(conv_shape),
+            room(proj_shape),
+            pltpu.SemaphoreType.DMA((4,)),
+            pltpu.SemaphoreType.DMA((7,)),
+        ],
+        compiler_params=pltpu.CompilerParams(vmem_limit_bytes=KERNEL_VMEM),
+    )(*made)
 
 
 def fits_fused(mesh):
     n_seq, n_dp = mesh.shape["seq"], mesh.shape["dp"]
-    return n_seq in (2, 4, 8) and n_dp == 4
+    return n_seq == 8 and n_dp == 4
 
 
 def solution(mesh):

time: 65.7 us -> 67.5 us (1.027)
  Pallas kernels: 53.2 us -> 66.7 us
  local copies, waits for them, and re-layouts: 11.4 us -> 0 us
    unnamed x23 -> x0, local copies, waits for them, and re-layouts: 11.4 us -> none
    pallas_call x1, Pallas kernels: 53.2 us -> 64.4 us  [per_device_fused(): pl.pallas_call(functools.partial(tower_kernel, n_seq, n_dp, scale), out_s...]
    pallas_call x0 -> x1, Pallas kernels: none -> 2.21 us  [per_device_fused(): pl.pallas_call(store_kernel, out_shape=shapes, in_specs=[hbm] * 4, out_sp...]
where the time goes in v2:
time: 67.5 us; the launch traced here: 67.3 us
  Pallas kernels  66.7 us (99%)
    pallas_call x1, Pallas kernels, per_device_fused(): pl.pallas_call(functools.partial(tower_kernel, n_seq, n_dp, scale), out_s...  64.4 us
    pallas_call x1, Pallas kernels, per_device_fused(): pl.pallas_call(store_kernel, out_shape=shapes, in_specs=[hbm] * 4, out_sp...  2.21 us

profile of v2, /device:TPU:1, one launch (start us, length us, event | category | flops | bytes accessed | tf_op | source)
XLA Modules:
  0.0 67.3 jit_solution(9104893876409238584)
XLA Ops:
  0.6 64.4 %shard_map.135 = (bf16[1,192,128]{2,1,0:T(8,128)(2,1)}, f32[1,4,2048]{2,1,0:T(4,128)}, f32[192,256]{1,0:T(8,128)}, bf16[4,8,64,128]{3,2,1,0:T(8,128)(2,1)}) custom-call(s32[1,2048]{1,0:T(1,128)} %bases_in.1, bf16[60,256]{1,0:T(8,128)(2,1)} %stem_in.1, bf16[3,256,128]{2,1,0:T(8,128)(2,1)} %conv1_in.1, bf16[128,256]{1,0:T(8,128)(2,1)} %proj1_in.1, ...), custom_call_target="tpu_custom_call" | custom-call | tf_op jit(solution)/shard_map/pallas_call | solution.py:708
  65.1 2.2 %shard_map.136 = (bf16[1,192,128]{2,1,0:T(8,128)(2,1)}, f32[1,4,2048]{2,1,0:T(4,128)}, f32[3,256,128]{2,1,0:T(8,128)}, f32[128,256]{1,0:T(8,128)}, f32[3,256,128...) custom-call(bf16[1,192,128]{2,1,0:T(8,128)(2,1)} %get-tuple-element.11.refs_0_, ...), custom_call_target="tpu_custom_call" | custom-call | tf_op jit(solution)/shard_map/pallas_call | solution.py:783

commit v3 on v1

--- a/solution.py
+++ b/solution.py
@@ -588,6 +588,18 @@
     reduce_end(1, one, conv1_out, proj1_out)
 
 
+def store_kernel(*refs):
+    sems = refs[-1]
+    count = (len(refs) - 1) // 2
+    copies = [
+        pltpu.make_async_copy(refs[i], refs[count + i], sems.at[i]) for i in range(count)
+    ]
+    for copy in copies:
+        copy.start()
+    for copy in copies:
+        copy.wait()
+
+
 def per_device_fused(
     bases,
     stem_table,
@@ -610,7 +622,7 @@
     vmem = pl.BlockSpec(memory_space=pltpu.VMEM)
     sds = jax.ShapeDtypeStruct
     piece = width // n_seq
-    return pl.pallas_call(
+    made = pl.pallas_call(
         functools.partial(tower_kernel, n_seq, n_dp, scale),
         out_shape=(
             sds((1, chans, cotangent.shape[2]), BF16),
@@ -674,6 +686,14 @@
         bin_weight,
         cotangent,
     )
+    return pl.pallas_call(
+        store_kernel,
+        out_shape=tuple(sds(leaf.shape, leaf.dtype) for leaf in made),
+        in_specs=[vmem] * len(made),
+        out_specs=(pl.BlockSpec(memory_space=pl.ANY),) * len(made),
+        scratch_shapes=[pltpu.SemaphoreType.DMA((len(made),))],
+        compiler_params=pltpu.CompilerParams(vmem_limit_bytes=2 * 1024 * 1024),
+    )(*made)
 
 
 def fits_fused(mesh):

time: 65.7 us -> 62.1 us (0.945)
  local copies, waits for them, and re-layouts: 11.4 us -> 6.67 us
  Pallas kernels: 53.2 us -> 54.4 us
    unnamed x23 -> x16, local copies, waits for them, and re-layouts: 11.4 us -> 6.67 us
    pallas_call x0 -> x1, Pallas kernels: none -> 1.11 us  [per_device_fused(): pl.pallas_call(store_kernel, out_shape=tuple((sds(leaf.shape, leaf.dtype)...]
where the time goes in v3:
time: 62.1 us; the launch traced here: 61.7 us
  Pallas kernels  54.4 us (88%)
  local copies, waits for them, and re-layouts  6.67 us (11%)
  between operations  0.66 us (1%)
    pallas_call x1, Pallas kernels, per_device_fused(): pl.pallas_call(functools.partial(tower_kernel, n_seq, n_dp, scale), out_s...  53.2 us
    unnamed x16, local copies, waits for them, and re-layouts  6.67 us

profile of v3, /device:TPU:1, one launch (start us, length us, event | category | flops | bytes accessed | tf_op | source)
XLA Modules:
  0.0 61.7 jit_solution(2607966414220149788)
XLA Ops:
  0.6 0.0 copy-start
  0.6 0.9 %copy-done = bf16[3,256,128]{2,1,0:T(8,128)(2,1)S(1)} copy-done((bf16[3,256,128]{2,1,0:T(8,128)(2,1)S(1)}, bf16[3,256,128]{2,1,0:T(8,128)(2,1)}, u32[]{:S(2)}) %copy-start) | copy-done | bytes 196632
  1.6 0.0 copy-start.1
  1.6 0.9 %copy-done.1 = bf16[3,256,128]{2,1,0:T(8,128)(2,1)S(1)} copy-done((bf16[3,256,128]{2,1,0:T(8,128)(2,1)S(1)}, bf16[3,256,128]{2,1,0:T(8,128)(2,1)}, u32[]{:S(2)}) %copy-start.1) | copy-done | bytes 196632
  2.5 0.0 copy-start.2
  2.5 0.9 %copy-done.2 = bf16[192,256]{1,0:T(8,128)(2,1)S(1)} copy-done((bf16[192,256]{1,0:T(8,128)(2,1)S(1)}, bf16[192,256]{1,0:T(8,128)(2,1)}, u32[]{:S(2)}) %copy-start.2) | copy-done | bytes 98328
  3.4 0.0 copy-start.3
  3.4 0.8 %copy-done.3 = bf16[128,256]{1,0:T(8,128)(2,1)S(1)} copy-done((bf16[128,256]{1,0:T(8,128)(2,1)S(1)}, bf16[128,256]{1,0:T(8,128)(2,1)}, u32[]{:S(2)}) %copy-start.3) | copy-done | bytes 65560
  4.2 0.0 copy-start.4
  4.2 0.8 %copy-done.4 = bf16[128,256]{1,0:T(8,128)(2,1)S(1)} copy-done((bf16[128,256]{1,0:T(8,128)(2,1)S(1)}, bf16[128,256]{1,0:T(8,128)(2,1)}, u32[]{:S(2)}) %copy-start.4) | copy-done | bytes 65560
  5.1 0.0 copy-start.5
  5.1 0.8 %copy-done.5 = bf16[1,192,128]{2,1,0:T(8,128)(2,1)S(1)} copy-done((bf16[1,192,128]{2,1,0:T(8,128)(2,1)S(1)}, bf16[1,192,128]{2,1,0:T(8,128)(2,1)}, u32[]{:S(2)}) %copy-start.5) | copy-done | bytes 49176
  5.9 0.0 copy-start.6
  5.9 0.8 %copy-done.6 = bf16[60,256]{1,0:T(8,128)(2,1)S(1)} copy-done((bf16[60,256]{1,0:T(8,128)(2,1)S(1)}, bf16[60,256]{1,0:T(8,128)(2,1)}, u32[]{:S(2)}) %copy-start.6) | copy-done | bytes 30744
  6.6 0.0 copy-start.7
  6.6 0.7 %copy-done.7 = s32[1,2048]{1,0:T(1,128)S(1)} copy-done((s32[1,2048]{1,0:T(1,128)S(1)}, s32[1,2048]{1,0:T(1,128)}, u32[]{:S(2)}) %copy-start.7) | copy-done | bytes 8216
  7.3 53.2 %shard_map.135 = (bf16[1,192,128]{2,1,0:T(8,128)(2,1)S(1)}, f32[1,4,2048]{2,1,0:T(4,128)S(1)}, f32[3,256,128]{2,1,0:T(8,128)S(1)}, f32[128,256]{1,0:T(8,128)S(1)...) custom-call(s32[1,2048]{1,0:T(1,128)S(1)} %copy-done.7, ...), custom_call_target="tpu_custom_call" | custom-call | tf_op jit(solution)/shard_map/pallas_call | solution.py:625
  60.6 1.1 %shard_map.136 = (bf16[1,192,128]{2,1,0:T(8,128)(2,1)}, f32[1,4,2048]{2,1,0:T(4,128)}, f32[3,256,128]{2,1,0:T(8,128)}, f32[128,256]{1,0:T(8,128)}, f32[3,256,128...) custom-call(bf16[1,192,128]{2,1,0:T(8,128)(2,1)S(1)} %get-tuple-element.14.refs_0_, ...), custom_call_target="tpu_custom_call" | custom-call | tf_op jit(solution)/shard_map/pallas_call | solution.py:689
Async XLA Ops:
  0.6 0.9 %copy-start = (bf16[3,256,128]{2,1,0:T(8,128)(2,1)S(1)}, bf16[3,256,128]{2,1,0:T(8,128)(2,1)}, u32[]{:S(2)}) copy-start(bf16[3,256,128]{2,1,0:T(8,128)(2,1)} %conv1_ref.1) | copy-start | bytes 589828
  1.6 0.9 %copy-start.1 = (bf16[3,256,128]{2,1,0:T(8,128)(2,1)S(1)}, bf16[3,256,128]{2,1,0:T(8,128)(2,1)}, u32[]{:S(2)}) copy-start(bf16[3,256,128]{2,1,0:T(8,128)(2,1)} %conv2_ref.1) | copy-start | bytes 589828
  2.5 0.9 %copy-start.2 = (bf16[192,256]{1,0:T(8,128)(2,1)S(1)}, bf16[192,256]{1,0:T(8,128)(2,1)}, u32[]{:S(2)}) copy-start(bf16[192,256]{1,0:T(8,128)(2,1)} %binw_ref.1) | copy-start | bytes 294916
  3.4 0.8 %copy-start.3 = (bf16[128,256]{1,0:T(8,128)(2,1)S(1)}, bf16[128,256]{1,0:T(8,128)(2,1)}, u32[]{:S(2)}) copy-start(bf16[128,256]{1,0:T(8,128)(2,1)} %proj1_ref.1) | copy-start | bytes 196612
  4.2 0.8 %copy-start.4 = (bf16[128,256]{1,0:T(8,128)(2,1)S(1)}, bf16[128,256]{1,0:T(8,128)(2,1)}, u32[]{:S(2)}) copy-start(bf16[128,256]{1,0:T(8,128)(2,1)} %proj2_ref.1) | copy-start | bytes 196612
  5.1 0.8 %copy-start.5 = (bf16[1,192,128]{2,1,0:T(8,128)(2,1)S(1)}, bf16[1,192,128]{2,1,0:T(8,128)(2,1)}, u32[]{:S(2)}) copy-start(bf16[1,192,128]{2,1,0:T(8,128)(2,1)} %cot_ref.1) | copy-start | bytes 147460
  5.9 0.8 %copy-start.6 = (bf16[60,256]{1,0:T(8,128)(2,1)S(1)}, bf16[60,256]{1,0:T(8,128)(2,1)}, u32[]{:S(2)}) copy-start(bf16[60,256]{1,0:T(8,128)(2,1)} %stem_ref.1) | copy-start | bytes 92164
  6.6 0.7 %copy-start.7 = (s32[1,2048]{1,0:T(1,128)S(1)}, s32[1,2048]{1,0:T(1,128)}, u32[]{:S(2)}) copy-start(s32[1,2048]{1,0:T(1,128)} %bases_ref.1) | copy-start | bytes 24580
